TPU v7x, 256 devices: a whole 4x4x8 slice. The times are simulated.
256 devices in a mesh: layer: 8 (over y, core), unit: 32 (over x, z).
Axes of the slice: x: 4, y: 4, z: 8, core: 2. Of those that a mesh axis runs over, the one named last changes fastest.
Arguments:
- tokens: int32 [4, 32], replicated, may hold values from 0 to 255
- embed: bfloat16 [256, 8192], P(None, 'unit'), may hold values from -6 to 6
- weights: bfloat16 [8, 128, 32, 64, 256], P('layer', 'unit'), may hold values from -0.125 to 0.125
- layout: int32 [8, 128, 32], P('layer', 'unit'), may hold values from 0 to 255, as said below
- bias: float32 [8, 128, 256], P('layer', 'unit'), may hold values from -4 to 4
- d_hidden: bfloat16 [8, 4, 32, 8192], P('layer', None, None, 'unit'), may hold values from -6 to 6
Outputs:
- hidden: bfloat16 [8, 4, 32, 8192], P('layer', None, None, 'unit')
- grad_weights: bfloat16 [8, 128, 32, 64, 256], P('layer', 'unit')
- grad_bias: float32 [8, 128, 256], P('layer', 'unit')
Inputs may be any that keep to these rules, and one draw needn't show every extreme that they name: The 32 entries of every row layout[l, j] are distinct and rising; numbers under 128 are blocks of the layer's input, the others of its own previous hidden state.
All inputs are finite; a program needn't handle non-finite values.
Results may differ from a plain program's by a relative error of at most 0.0085.
Values may be sent and summed in bfloat16 or wider, within the bound.
No kernel may reach another device: no remote copies, remote signals or barrier semaphores. Data moves between devices by JAX's collectives and lax.ppermute only.
A program may use at most 64 MiB of HBM per device.

v0:
```python
import jax
import jax.numpy as jnp
from jax import lax
from jax.sharding import Mesh
from jax.sharding import PartitionSpec as P

UNIT = ("unit_0", "unit_1")


def joined_along(pieces, dim):
    pieces = jnp.moveaxis(pieces, 0, dim)
    lengths = pieces.shape
    return pieces.reshape(*lengths[:dim], lengths[dim] * lengths[dim + 1], *lengths[dim + 2 :])


def all_blocks_2(value, axes, turns):
    pieces = value
    for k in turns:
        pieces = lax.all_gather(pieces, axes[k])
    done = turns[::-1]
    back = [done.index(k) for k in range(len(axes))]
    pieces = pieces.transpose(*back, *range(len(axes), pieces.ndim))
    return pieces.reshape(-1, *value.shape)


def whole_of(value, axes, turns, dim):
    return joined_along(all_blocks_2(value, axes, turns), dim)


def copy_for_each(value, axis):
    count = lax.axis_size(axis)
    return lax.all_to_all(
        jnp.broadcast_to(value[None], (count, *value.shape)), axis, 0, 0, tiled=True
    )


def collect(value, axis, dim):
    pieces = copy_for_each(value, axis)
    return joined_along(pieces, dim)


def passed_along(value, axis, steps):
    count = lax.axis_size(axis)
    leading, last = (max(0, -steps), min(count, count - steps))
    return lax.ppermute(value, axis, [(source, source + steps) for source in range(leading, last)])


def in_blocks(value, dim, count):
    lengths = value.shape
    pieces = value.reshape(*lengths[:dim], count, lengths[dim] // count, *lengths[dim + 1 :])
    return jnp.moveaxis(pieces, dim, 0)


def summed_on_arrival(value, axis, dim):
    count = lax.axis_size(axis)
    pieces = lax.all_to_all(in_blocks(value, dim, count), axis, 0, 0, tiled=True)
    return jnp.sum(pieces.astype(jnp.float32), axis=0)


def gate_math(pre_act, cell_prev):
    gate_size = pre_act.shape[-1] // 4
    in_gate = jax.nn.sigmoid(pre_act[..., :gate_size])
    forget = jax.nn.sigmoid(pre_act[..., gate_size : 2 * gate_size])
    update = jnp.tanh(pre_act[..., 2 * gate_size : 3 * gate_size])
    out_gate = jax.nn.sigmoid(pre_act[..., 3 * gate_size :])
    cell_state = forget * cell_prev + in_gate * update
    new_hidden = (out_gate * jnp.tanh(cell_state)).astype(jnp.bfloat16)
    return (jnp.concatenate([in_gate, forget, update, out_gate], -1), cell_state, new_hidden)


def gate_grads(gate_acts, cell_state, cell_prev, grad_hidden, grad_carry):
    gate_size = gate_acts.shape[-1] // 4
    in_gate = gate_acts[..., :gate_size]
    forget = gate_acts[..., gate_size : 2 * gate_size]
    update = gate_acts[..., 2 * gate_size : 3 * gate_size]
    out_gate = gate_acts[..., 3 * gate_size :]
    squash = jnp.tanh(cell_state)
    grad_cell = grad_carry + grad_hidden * out_gate * (1.0 - squash * squash)
    grad_in = grad_cell * update * in_gate * (1.0 - in_gate)
    grad_forget = grad_cell * cell_prev * forget * (1.0 - forget)
    grad_update = grad_cell * in_gate * (1.0 - update * update)
    grad_out = grad_hidden * squash * out_gate * (1.0 - out_gate)
    grad_pre = jnp.concatenate([grad_in, grad_forget, grad_update, grad_out], -1).astype(
        jnp.bfloat16
    )
    return (grad_pre, grad_cell * forget)


def to_blocks(rows_arr):
    return rows_arr.transpose(1, 0, 2).reshape(
        rows_arr.shape[1], rows_arr.shape[0] * rows_arr.shape[2]
    )


def from_blocks(block_arr, batch_rows, block_size):
    return block_arr.reshape(block_arr.shape[0], batch_rows, block_size).transpose(1, 0, 2)


def on_device(tokens, embed, weights, layout, bias, d_hidden):
    layer_count = lax.axis_size("layer")
    layer_idx = lax.axis_index("layer")
    unit_count = lax.axis_size(UNIT)
    step_count, batch_rows = tokens.shape
    vocab_size, unit_width = embed.shape
    weight_blocks = weights[0]
    layout_rows = layout[0]
    bias_rows = bias[0]
    cotangent = d_hidden[0]
    own_blocks, nonzero, block_size, gate_width = weight_blocks.shape
    full_width = unit_width * unit_count
    all_blocks = full_width // block_size
    wave_count = step_count + layer_count - 1
    row_width = batch_rows * block_size
    vocab_ids = jnp.arange(vocab_size, dtype=jnp.int32)
    flat_layout = layout_rows.reshape(-1)
    full_table = whole_of(embed, UNIT, (0, 1), 1).reshape(vocab_size, all_blocks, block_size)

    def lookup(time_step, table3):
        ids_row = lax.dynamic_index_in_dim(tokens, time_step, 0, False)
        onehot = (ids_row[:, None] == vocab_ids[None, :]).astype(jnp.bfloat16)
        looked = jnp.einsum("bv,vjc->jbc", onehot, table3, preferred_element_type=jnp.float32)
        return looked.astype(jnp.bfloat16).reshape(table3.shape[1], row_width)

    def forward_wave(wave_idx, loop_state):
        hidden_own, cell_state, stored, cell_log, act_log, hidden_log = loop_state
        time_step = wave_idx - layer_idx
        in_range = (time_step >= 0) & (time_step < step_count)
        clipped = jnp.clip(time_step, 0, step_count - 1)
        slot = jnp.where(in_range, time_step, step_count)
        hidden_full = collect(hidden_own, UNIT, 0)
        below_full = passed_along(hidden_full, "layer", 1)
        source_full = jnp.where(layer_idx == 0, lookup(clipped, full_table), below_full)
        inputs = jnp.concatenate([source_full, hidden_full], 0)
        picked = jnp.take(inputs, flat_layout, axis=0).reshape(
            own_blocks, nonzero, batch_rows, block_size
        )
        pre_act = (
            jnp.einsum("jkbc,jkcd->bjd", picked, weight_blocks, preferred_element_type=jnp.float32)
            + bias_rows
        )
        gate_acts, new_cell, new_hidden = gate_math(pre_act, cell_state)
        hidden_own = jnp.where(in_range, to_blocks(new_hidden), hidden_own)
        cell_state = jnp.where(in_range, new_cell, cell_state)
        stored = lax.dynamic_update_index_in_dim(stored, inputs, slot, 0)
        cell_log = lax.dynamic_update_index_in_dim(cell_log, new_cell, slot, 0)
        act_log = lax.dynamic_update_index_in_dim(act_log, gate_acts, slot, 0)
        hidden_log = lax.dynamic_update_index_in_dim(
            hidden_log, new_hidden.reshape(batch_rows, unit_width), slot, 0
        )
        return (hidden_own, cell_state, stored, cell_log, act_log, hidden_log)

    start = (
        jnp.zeros((own_blocks, row_width), jnp.bfloat16),
        jnp.zeros((batch_rows, own_blocks, block_size), jnp.float32),
        jnp.zeros((step_count + 1, 2 * all_blocks, row_width), jnp.bfloat16),
        jnp.zeros((step_count + 1, batch_rows, own_blocks, block_size), jnp.float32),
        jnp.zeros((step_count + 1, batch_rows, own_blocks, gate_width), jnp.float32),
        jnp.zeros((step_count + 1, batch_rows, unit_width), jnp.bfloat16),
    )
    _, _, stored, cell_log, act_log, hidden_log = lax.fori_loop(0, wave_count, forward_wave, start)

    def backward_wave(wave_idx, loop_state):
        send_down, grad_recur, grad_carry, pre_log = loop_state
        time_step = step_count - 1 - wave_idx + (layer_count - 1 - layer_idx)
        in_range = (time_step >= 0) & (time_step < step_count)
        clipped = jnp.clip(time_step, 0, step_count - 1)
        slot = jnp.where(in_range, time_step, step_count)
        from_above = passed_along(send_down.astype(jnp.bfloat16), "layer", -1).astype(
            send_down.dtype
        )
        upstream = lax.dynamic_index_in_dim(cotangent, clipped, 0, False).astype(jnp.float32)
        grad_hidden = (
            upstream.reshape(batch_rows, own_blocks, block_size)
            + from_blocks(from_above, batch_rows, block_size)
            + grad_recur
        )
        gate_acts = lax.dynamic_index_in_dim(act_log, clipped, 0, False)
        cell_state = lax.dynamic_index_in_dim(cell_log, clipped, 0, False)
        prev_index = jnp.maximum(clipped - 1, 0)
        cell_prev = lax.dynamic_index_in_dim(cell_log, prev_index, 0, False) * (clipped > 0).astype(
            jnp.float32
        )
        grad_pre, carry_new = gate_grads(gate_acts, cell_state, cell_prev, grad_hidden, grad_carry)
        contrib = jnp.einsum(
            "bjd,jkcd->jkbc", grad_pre, weight_blocks, preferred_element_type=jnp.float32
        )
        partial_value = (
            jnp.zeros((2 * all_blocks, row_width), jnp.float32)
            .at[flat_layout]
            .add(contrib.reshape(own_blocks * nonzero, row_width))
        )
        halves = partial_value.reshape(2, all_blocks, row_width)
        summed = summed_on_arrival(halves.astype(jnp.bfloat16), UNIT, 1)
        source_sum = summed[0]
        recur_sum = summed[1]
        send_down = jnp.where(in_range, source_sum, jnp.zeros_like(send_down))
        grad_recur = jnp.where(in_range, from_blocks(recur_sum, batch_rows, block_size), grad_recur)
        grad_carry = jnp.where(in_range, carry_new, grad_carry)
        pre_log = lax.dynamic_update_index_in_dim(pre_log, grad_pre, slot, 0)
        return (send_down, grad_recur, grad_carry, pre_log)

    start = (
        jnp.zeros((own_blocks, row_width), jnp.float32),
        jnp.zeros((batch_rows, own_blocks, block_size), jnp.float32),
        jnp.zeros((batch_rows, own_blocks, block_size), jnp.float32),
        jnp.zeros((step_count + 1, batch_rows, own_blocks, gate_width), jnp.bfloat16),
    )
    _, _, _, pre_log = lax.fori_loop(0, wave_count, backward_wave, start)
    pre_used = pre_log[:step_count]
    picked_all = jnp.take(stored[:step_count], flat_layout, axis=1).reshape(
        step_count, own_blocks, nonzero, batch_rows, block_size
    )
    grad_w = jnp.einsum(
        "sjkbc,sbjd->jkcd", picked_all, pre_used, preferred_element_type=jnp.float32
    ).astype(jnp.bfloat16)
    grad_b = jnp.sum(pre_used.astype(jnp.float32), axis=(0, 1))
    return (hidden_log[:step_count][None], grad_w[None], grad_b[None])


def solution(mesh):
    torus = Mesh(mesh.devices.reshape(mesh.shape["layer"], 4, 8), ("layer", "unit_0", "unit_1"))
    return jax.shard_map(
        on_device,
        mesh=torus,
        in_specs=(
            P(),
            P(None, UNIT),
            P("layer", UNIT, None, None, None),
            P("layer", UNIT, None),
            P("layer", UNIT, None),
            P("layer", None, None, UNIT),
        ),
        out_specs=(
            P("layer", None, None, UNIT),
            P("layer", UNIT, None, None, None),
            P("layer", UNIT, None),
        ),
        check_vma=False,
    )
```

profile of v0, /device:TPU:41, one launch (start us, length us, event | category | flops | bytes accessed | tf_op | source)
XLA Modules:
  0.0 1106.9 jit_solution(3861603854480420609)
XLA Ops:
  7.2 12.2 %all-gather = bf16[1024,256]{1,0:T(8,128)(2,1)} all-gather(bf16[256,256]{1,0:T(8,128)(2,1)} %param.11), channel_id=2, replica_groups=mesh['layer'=8,'unit_0'=4,'unit_1'=8] {'unit_0'}, dimensions={0}, use_global_device_ids=true | all-gather | bytes 655360 | tf_op jit(solution)/shard_map/all_gather | solution.py:19
  21.7 54.4 %all-gather.4.cloned.1.call-done = bf16[32,256,256]{2,1,0:T(8,128)(2,1)} async-done(((bf16[4,256,256]{2,1,0:T(8,128)(2,1)}), bf16[32,256,256]{2,1,0:T(8,128)(2,1)}) %all-gather.4.cloned.1.call-update) | async-done | bytes 4194320 | tf_op jit(solution)/shard_map/all_gather | solution.py:19
  80.8 6.4 copy.43
  87.2 6.8 copy.44
  98.0 426.3 %while.47 = (s32[]{:T(128)}, bf16[4,2048]{1,0:T(4,128)(2,1)S(1)}, f32[32,4,64]{2,0,1:T(8,128)S(1)}, bf16[5,256,2048]{2,1,0:T(8,128)(2,1)}, f32[5,32,4,64]{3,1,2,...) while((s32[]{:T(128)}, bf16[4,2048]{1,0:T(4,128)(2,1)S(1)}, ...), condition=%wide.region_1.2_spmd.clone, body=%wide.region_0.1_spmd.clone.sunk | while | flops 273770624 | bytes 26046972 | solution.py:160
  99.1 8.6 all-to-all-start
  112.0 11.7 %all-to-all-done = bf16[32,4,2048]{2,1,0:T(4,128)(2,1)S(1)} async-done(((bf16[32,4,2048]{2,1,0:T(4,128)(2,1)}), bf16[32,4,2048]{2,1,0:T(4,128)(2,1)S(1)}, u32[]{:S(2)}, u32[]{:S(2)}) %all-to-all-start) | async-done | bytes 524320 | tf_op jit(solution)/shard_map/while/body/eval_jaxpr/all_to_all | solution.py:32
  129.8 6.1 collective-permute-done
  153.0 11.5 %all-to-all-done = bf16[32,4,2048]{2,1,0:T(4,128)(2,1)S(1)} async-done(((bf16[32,4,2048]{2,1,0:T(4,128)(2,1)}), bf16[32,4,2048]{2,1,0:T(4,128)(2,1)S(1)}, u32[]{:S(2)}, u32[]{:S(2)}) %all-to-all-start) | async-done | bytes 524320 | tf_op jit(solution)/shard_map/while/body/eval_jaxpr/all_to_all | solution.py:32
  170.5 6.1 collective-permute-done
  193.8 11.3 %all-to-all-done = bf16[32,4,2048]{2,1,0:T(4,128)(2,1)S(1)} async-done(((bf16[32,4,2048]{2,1,0:T(4,128)(2,1)}), bf16[32,4,2048]{2,1,0:T(4,128)(2,1)S(1)}, u32[]{:S(2)}, u32[]{:S(2)}) %all-to-all-start) | async-done | bytes 524320 | tf_op jit(solution)/shard_map/while/body/eval_jaxpr/all_to_all | solution.py:32
  209.2 6.1 collective-permute-done
  232.1 8.9 all-to-all-done
  247.0 6.1 collective-permute-done
  270.1 8.5 all-to-all-done
  278.7 6.1 collective-permute-start
  284.9 6.1 collective-permute-done
  307.8 8.6 all-to-all-done
  316.6 6.0 collective-permute-start
  322.6 6.1 collective-permute-done
  345.5 8.3 all-to-all-done
  353.9 6.4 collective-permute-start
  360.3 6.1 collective-permute-done
  383.2 8.3 all-to-all-done
  391.6 6.3 collective-permute-start
  398.0 6.1 collective-permute-done
  420.8 8.3 all-to-all-done
  429.3 6.2 collective-permute-start
  435.5 6.1 collective-permute-done
  458.4 8.3 all-to-all-done
  466.9 6.1 collective-permute-start
  473.1 6.1 collective-permute-done
  496.0 8.3 all-to-all-done
  504.5 6.1 collective-permute-start
  510.6 6.1 collective-permute-done
  544.0 547.8 %while.48 = (s32[]{:T(128)}, bf16[4,2048]{1,0:T(4,128)(2,1)S(1)}, f32[32,4,64]{2,0,1:T(8,128)S(1)}, f32[32,4,64]{2,0,1:T(8,128)S(1)}, bf16[5,32,4,256]{3,1,0,2:T...) while((s32[]{:T(128)}, bf16[4,2048]{1,0:T(4,128)(2,1)S(1)}, ...), condition=%wide.region_5.6_spmd.clone, body=%wide.region_2.5_spmd.clone.sunk | while | flops 136855952 | bytes 23823848 | solution.py:208
  544.0 7.7 collective-permute-start.1
  568.2 27.9 %all-to-all-done.1 = bf16[32,2,4,2048]{3,2,1,0:T(4,128)(2,1)S(1)} async-done(((bf16[32,2,4,2048]{3,2,1,0:T(4,128)(2,1)}), bf16[32,2,4,2048]{3,2,1,0:T(4,128)(2,1)S(1)}, u32[]{:S(2)}, u32[]{:S(2)}) %all-to-all-start.1) | async-done | bytes 1048608 | tf_op jit(solution)/shard_map/while/body/eval_jaxpr/all_to_all | solution.py:56
  617.4 27.8 %all-to-all-done.1 = bf16[32,2,4,2048]{3,2,1,0:T(4,128)(2,1)S(1)} async-done(((bf16[32,2,4,2048]{3,2,1,0:T(4,128)(2,1)}), bf16[32,2,4,2048]{3,2,1,0:T(4,128)(2,1)S(1)}, u32[]{:S(2)}, u32[]{:S(2)}) %all-to-all-start.1) | async-done | bytes 1048608 | tf_op jit(solution)/shard_map/while/body/eval_jaxpr/all_to_all | solution.py:56
  667.1 28.0 %all-to-all-done.1 = bf16[32,2,4,2048]{3,2,1,0:T(4,128)(2,1)S(1)} async-done(((bf16[32,2,4,2048]{3,2,1,0:T(4,128)(2,1)}), bf16[32,2,4,2048]{3,2,1,0:T(4,128)(2,1)S(1)}, u32[]{:S(2)}, u32[]{:S(2)}) %all-to-all-start.1) | async-done | bytes 1048608 | tf_op jit(solution)/shard_map/while/body/eval_jaxpr/all_to_all | solution.py:56
  716.8 27.9 %all-to-all-done.1 = bf16[32,2,4,2048]{3,2,1,0:T(4,128)(2,1)S(1)} async-done(((bf16[32,2,4,2048]{3,2,1,0:T(4,128)(2,1)}), bf16[32,2,4,2048]{3,2,1,0:T(4,128)(2,1)S(1)}, u32[]{:S(2)}, u32[]{:S(2)}) %all-to-all-start.1) | async-done | bytes 1048608 | tf_op jit(solution)/shard_map/while/body/eval_jaxpr/all_to_all | solution.py:56
  766.3 27.9 %all-to-all-done.1 = bf16[32,2,4,2048]{3,2,1,0:T(4,128)(2,1)S(1)} async-done(((bf16[32,2,4,2048]{3,2,1,0:T(4,128)(2,1)}), bf16[32,2,4,2048]{3,2,1,0:T(4,128)(2,1)S(1)}, u32[]{:S(2)}, u32[]{:S(2)}) %all-to-all-start.1) | async-done | bytes 1048608 | tf_op jit(solution)/shard_map/while/body/eval_jaxpr/all_to_all | solution.py:56
  815.8 27.9 %all-to-all-done.1 = bf16[32,2,4,2048]{3,2,1,0:T(4,128)(2,1)S(1)} async-done(((bf16[32,2,4,2048]{3,2,1,0:T(4,128)(2,1)}), bf16[32,2,4,2048]{3,2,1,0:T(4,128)(2,1)S(1)}, u32[]{:S(2)}, u32[]{:S(2)}) %all-to-all-start.1) | async-done | bytes 1048608 | tf_op jit(solution)/shard_map/while/body/eval_jaxpr/all_to_all | solution.py:56
  865.3 27.9 %all-to-all-done.1 = bf16[32,2,4,2048]{3,2,1,0:T(4,128)(2,1)S(1)} async-done(((bf16[32,2,4,2048]{3,2,1,0:T(4,128)(2,1)}), bf16[32,2,4,2048]{3,2,1,0:T(4,128)(2,1)S(1)}, u32[]{:S(2)}, u32[]{:S(2)}) %all-to-all-start.1) | async-done | bytes 1048608 | tf_op jit(solution)/shard_map/while/body/eval_jaxpr/all_to_all | solution.py:56
  914.8 27.9 %all-to-all-done.1 = bf16[32,2,4,2048]{3,2,1,0:T(4,128)(2,1)S(1)} async-done(((bf16[32,2,4,2048]{3,2,1,0:T(4,128)(2,1)}), bf16[32,2,4,2048]{3,2,1,0:T(4,128)(2,1)S(1)}, u32[]{:S(2)}, u32[]{:S(2)}) %all-to-all-start.1) | async-done | bytes 1048608 | tf_op jit(solution)/shard_map/while/body/eval_jaxpr/all_to_all | solution.py:56
  964.3 27.9 %all-to-all-done.1 = bf16[32,2,4,2048]{3,2,1,0:T(4,128)(2,1)S(1)} async-done(((bf16[32,2,4,2048]{3,2,1,0:T(4,128)(2,1)}), bf16[32,2,4,2048]{3,2,1,0:T(4,128)(2,1)S(1)}, u32[]{:S(2)}, u32[]{:S(2)}) %all-to-all-start.1) | async-done | bytes 1048608 | tf_op jit(solution)/shard_map/while/body/eval_jaxpr/all_to_all | solution.py:56
  1013.8 27.9 %all-to-all-done.1 = bf16[32,2,4,2048]{3,2,1,0:T(4,128)(2,1)S(1)} async-done(((bf16[32,2,4,2048]{3,2,1,0:T(4,128)(2,1)}), bf16[32,2,4,2048]{3,2,1,0:T(4,128)(2,1)S(1)}, u32[]{:S(2)}, u32[]{:S(2)}) %all-to-all-start.1) | async-done | bytes 1048608 | tf_op jit(solution)/shard_map/while/body/eval_jaxpr/all_to_all | solution.py:56
  1063.3 27.9 %all-to-all-done.1 = bf16[32,2,4,2048]{3,2,1,0:T(4,128)(2,1)S(1)} async-done(((bf16[32,2,4,2048]{3,2,1,0:T(4,128)(2,1)}), bf16[32,2,4,2048]{3,2,1,0:T(4,128)(2,1)S(1)}, u32[]{:S(2)}, u32[]{:S(2)}) %all-to-all-start.1) | async-done | bytes 1048608 | tf_op jit(solution)/shard_map/while/body/eval_jaxpr/all_to_all | solution.py:56
  (601 shorter events, 474.3 us)
Async XLA Ops:
  7.2 69.0 %all-gather.4.cloned.1.call-start = ((), (), s32[]{:S(2)}) async-start(), calls=%async_computation.2 | async-start | bytes 4718592 | tf_op jit(solution)/shard_map/all_gather | solution.py:19
  99.1 24.5 %all-to-all-start = ((bf16[32,4,2048]{2,1,0:T(4,128)(2,1)}), bf16[32,4,2048]{2,1,0:T(4,128)(2,1)S(1)}, u32[]{:S(2)}, u32[]{:S(2)}) async-start(bf16[32,4,2048]{2,1,0:T(4,128)(2,1)} %broadcast_in_dim.161), calls=%async_computation | async-start | bytes 1048576 | tf_op jit(solution)/shard_map/while/body/eval_jaxpr/all_to_all | solution.py:32
  123.8 12.1 %collective-permute-start = (bf16[128,2048]{1,0:T(8,128)(2,1)S(1)}, bf16[128,2048]{1,0:T(8,128)(2,1)S(1)}, u32[]{:S(2)}, u32[]{:S(2)}) collective-permute-start(bf16[128,2048]{1,0:T(8,128)(2,1)S(1)} %reshape.332), channel_id=1, source_target_pairs={{0,32},{32,64},{64,96},{96,128},{128,160},{160,192},{192,224},{1,3... | collective-permute-start | bytes 1572872 | tf_op jit(solution)/shard_map/while/body/eval_jaxpr/ppermute | solution.py:45
  144.5 20.0 %all-to-all-start = ((bf16[32,4,2048]{2,1,0:T(4,128)(2,1)}), bf16[32,4,2048]{2,1,0:T(4,128)(2,1)S(1)}, u32[]{:S(2)}, u32[]{:S(2)}) async-start(bf16[32,4,2048]{2,1,0:T(4,128)(2,1)} %broadcast_in_dim.161), calls=%async_computation | async-start | bytes 1048576 | tf_op jit(solution)/shard_map/while/body/eval_jaxpr/all_to_all | solution.py:32
  164.6 12.0 %collective-permute-start = (bf16[128,2048]{1,0:T(8,128)(2,1)S(1)}, bf16[128,2048]{1,0:T(8,128)(2,1)S(1)}, u32[]{:S(2)}, u32[]{:S(2)}) collective-permute-start(bf16[128,2048]{1,0:T(8,128)(2,1)S(1)} %reshape.332), channel_id=1, source_target_pairs={{0,32},{32,64},{64,96},{96,128},{128,160},{160,192},{192,224},{1,3... | collective-permute-start | bytes 1572872 | tf_op jit(solution)/shard_map/while/body/eval_jaxpr/ppermute | solution.py:45
  185.2 19.9 %all-to-all-start = ((bf16[32,4,2048]{2,1,0:T(4,128)(2,1)}), bf16[32,4,2048]{2,1,0:T(4,128)(2,1)S(1)}, u32[]{:S(2)}, u32[]{:S(2)}) async-start(bf16[32,4,2048]{2,1,0:T(4,128)(2,1)} %broadcast_in_dim.161), calls=%async_computation | async-start | bytes 1048576 | tf_op jit(solution)/shard_map/while/body/eval_jaxpr/all_to_all | solution.py:32
  205.2 10.1 collective-permute-start
  224.0 17.1 %all-to-all-start = ((bf16[32,4,2048]{2,1,0:T(4,128)(2,1)}), bf16[32,4,2048]{2,1,0:T(4,128)(2,1)S(1)}, u32[]{:S(2)}, u32[]{:S(2)}) async-start(bf16[32,4,2048]{2,1,0:T(4,128)(2,1)} %broadcast_in_dim.161), calls=%async_computation | async-start | bytes 1048576 | tf_op jit(solution)/shard_map/while/body/eval_jaxpr/all_to_all | solution.py:32
  241.2 11.9 %collective-permute-start = (bf16[128,2048]{1,0:T(8,128)(2,1)S(1)}, bf16[128,2048]{1,0:T(8,128)(2,1)S(1)}, u32[]{:S(2)}, u32[]{:S(2)}) collective-permute-start(bf16[128,2048]{1,0:T(8,128)(2,1)S(1)} %reshape.332), channel_id=1, source_target_pairs={{0,32},{32,64},{64,96},{96,128},{128,160},{160,192},{192,224},{1,3... | collective-permute-start | bytes 1572872 | tf_op jit(solution)/shard_map/while/body/eval_jaxpr/ppermute | solution.py:45
  261.7 16.9 %all-to-all-start = ((bf16[32,4,2048]{2,1,0:T(4,128)(2,1)}), bf16[32,4,2048]{2,1,0:T(4,128)(2,1)S(1)}, u32[]{:S(2)}, u32[]{:S(2)}) async-start(bf16[32,4,2048]{2,1,0:T(4,128)(2,1)} %broadcast_in_dim.161), calls=%async_computation | async-start | bytes 1048576 | tf_op jit(solution)/shard_map/while/body/eval_jaxpr/all_to_all | solution.py:32
  278.7 12.2 %collective-permute-start = (bf16[128,2048]{1,0:T(8,128)(2,1)S(1)}, bf16[128,2048]{1,0:T(8,128)(2,1)S(1)}, u32[]{:S(2)}, u32[]{:S(2)}) collective-permute-start(bf16[128,2048]{1,0:T(8,128)(2,1)S(1)} %reshape.332), channel_id=1, source_target_pairs={{0,32},{32,64},{64,96},{96,128},{128,160},{160,192},{192,224},{1,3... | collective-permute-start | bytes 1572872 | tf_op jit(solution)/shard_map/while/body/eval_jaxpr/ppermute | solution.py:45
  299.7 16.7 %all-to-all-start = ((bf16[32,4,2048]{2,1,0:T(4,128)(2,1)}), bf16[32,4,2048]{2,1,0:T(4,128)(2,1)S(1)}, u32[]{:S(2)}, u32[]{:S(2)}) async-start(bf16[32,4,2048]{2,1,0:T(4,128)(2,1)} %broadcast_in_dim.161), calls=%async_computation | async-start | bytes 1048576 | tf_op jit(solution)/shard_map/while/body/eval_jaxpr/all_to_all | solution.py:32
  316.6 12.1 %collective-permute-start = (bf16[128,2048]{1,0:T(8,128)(2,1)S(1)}, bf16[128,2048]{1,0:T(8,128)(2,1)S(1)}, u32[]{:S(2)}, u32[]{:S(2)}) collective-permute-start(bf16[128,2048]{1,0:T(8,128)(2,1)S(1)} %reshape.332), channel_id=1, source_target_pairs={{0,32},{32,64},{64,96},{96,128},{128,160},{160,192},{192,224},{1,3... | collective-permute-start | bytes 1572872 | tf_op jit(solution)/shard_map/while/body/eval_jaxpr/ppermute | solution.py:45
  337.3 16.5 %all-to-all-start = ((bf16[32,4,2048]{2,1,0:T(4,128)(2,1)}), bf16[32,4,2048]{2,1,0:T(4,128)(2,1)S(1)}, u32[]{:S(2)}, u32[]{:S(2)}) async-start(bf16[32,4,2048]{2,1,0:T(4,128)(2,1)} %broadcast_in_dim.161), calls=%async_computation | async-start | bytes 1048576 | tf_op jit(solution)/shard_map/while/body/eval_jaxpr/all_to_all | solution.py:32
  353.9 12.5 %collective-permute-start = (bf16[128,2048]{1,0:T(8,128)(2,1)S(1)}, bf16[128,2048]{1,0:T(8,128)(2,1)S(1)}, u32[]{:S(2)}, u32[]{:S(2)}) collective-permute-start(bf16[128,2048]{1,0:T(8,128)(2,1)S(1)} %reshape.332), channel_id=1, source_target_pairs={{0,32},{32,64},{64,96},{96,128},{128,160},{160,192},{192,224},{1,3... | collective-permute-start | bytes 1572872 | tf_op jit(solution)/shard_map/while/body/eval_jaxpr/ppermute | solution.py:45
  375.1 16.4 %all-to-all-start = ((bf16[32,4,2048]{2,1,0:T(4,128)(2,1)}), bf16[32,4,2048]{2,1,0:T(4,128)(2,1)S(1)}, u32[]{:S(2)}, u32[]{:S(2)}) async-start(bf16[32,4,2048]{2,1,0:T(4,128)(2,1)} %broadcast_in_dim.161), calls=%async_computation | async-start | bytes 1048576 | tf_op jit(solution)/shard_map/while/body/eval_jaxpr/all_to_all | solution.py:32
  391.6 12.4 %collective-permute-start = (bf16[128,2048]{1,0:T(8,128)(2,1)S(1)}, bf16[128,2048]{1,0:T(8,128)(2,1)S(1)}, u32[]{:S(2)}, u32[]{:S(2)}) collective-permute-start(bf16[128,2048]{1,0:T(8,128)(2,1)S(1)} %reshape.332), channel_id=1, source_target_pairs={{0,32},{32,64},{64,96},{96,128},{128,160},{160,192},{192,224},{1,3... | collective-permute-start | bytes 1572872 | tf_op jit(solution)/shard_map/while/body/eval_jaxpr/ppermute | solution.py:45
  412.7 16.4 %all-to-all-start = ((bf16[32,4,2048]{2,1,0:T(4,128)(2,1)}), bf16[32,4,2048]{2,1,0:T(4,128)(2,1)S(1)}, u32[]{:S(2)}, u32[]{:S(2)}) async-start(bf16[32,4,2048]{2,1,0:T(4,128)(2,1)} %broadcast_in_dim.161), calls=%async_computation | async-start | bytes 1048576 | tf_op jit(solution)/shard_map/while/body/eval_jaxpr/all_to_all | solution.py:32
  429.3 12.3 %collective-permute-start = (bf16[128,2048]{1,0:T(8,128)(2,1)S(1)}, bf16[128,2048]{1,0:T(8,128)(2,1)S(1)}, u32[]{:S(2)}, u32[]{:S(2)}) collective-permute-start(bf16[128,2048]{1,0:T(8,128)(2,1)S(1)} %reshape.332), channel_id=1, source_target_pairs={{0,32},{32,64},{64,96},{96,128},{128,160},{160,192},{192,224},{1,3... | collective-permute-start | bytes 1572872 | tf_op jit(solution)/shard_map/while/body/eval_jaxpr/ppermute | solution.py:45
  450.2 16.6 %all-to-all-start = ((bf16[32,4,2048]{2,1,0:T(4,128)(2,1)}), bf16[32,4,2048]{2,1,0:T(4,128)(2,1)S(1)}, u32[]{:S(2)}, u32[]{:S(2)}) async-start(bf16[32,4,2048]{2,1,0:T(4,128)(2,1)} %broadcast_in_dim.161), calls=%async_computation | async-start | bytes 1048576 | tf_op jit(solution)/shard_map/while/body/eval_jaxpr/all_to_all | solution.py:32
  466.9 12.2 %collective-permute-start = (bf16[128,2048]{1,0:T(8,128)(2,1)S(1)}, bf16[128,2048]{1,0:T(8,128)(2,1)S(1)}, u32[]{:S(2)}, u32[]{:S(2)}) collective-permute-start(bf16[128,2048]{1,0:T(8,128)(2,1)S(1)} %reshape.332), channel_id=1, source_target_pairs={{0,32},{32,64},{64,96},{96,128},{128,160},{160,192},{192,224},{1,3... | collective-permute-start | bytes 1572872 | tf_op jit(solution)/shard_map/while/body/eval_jaxpr/ppermute | solution.py:45
  487.8 16.5 %all-to-all-start = ((bf16[32,4,2048]{2,1,0:T(4,128)(2,1)}), bf16[32,4,2048]{2,1,0:T(4,128)(2,1)S(1)}, u32[]{:S(2)}, u32[]{:S(2)}) async-start(bf16[32,4,2048]{2,1,0:T(4,128)(2,1)} %broadcast_in_dim.161), calls=%async_computation | async-start | bytes 1048576 | tf_op jit(solution)/shard_map/while/body/eval_jaxpr/all_to_all | solution.py:32
  504.5 12.2 %collective-permute-start = (bf16[128,2048]{1,0:T(8,128)(2,1)S(1)}, bf16[128,2048]{1,0:T(8,128)(2,1)S(1)}, u32[]{:S(2)}, u32[]{:S(2)}) collective-permute-start(bf16[128,2048]{1,0:T(8,128)(2,1)S(1)} %reshape.332), channel_id=1, source_target_pairs={{0,32},{32,64},{64,96},{96,128},{128,160},{160,192},{192,224},{1,3... | collective-permute-start | bytes 1572872 | tf_op jit(solution)/shard_map/while/body/eval_jaxpr/ppermute | solution.py:45
  544.0 9.5 collective-permute-start.1
  563.6 32.5 %all-to-all-start.1 = ((bf16[32,2,4,2048]{3,2,1,0:T(4,128)(2,1)}), bf16[32,2,4,2048]{3,2,1,0:T(4,128)(2,1)S(1)}, u32[]{:S(2)}, u32[]{:S(2)}) async-start(bf16[32,2,4,2048]{3,2,1,0:T(4,128)(2,1)} %copy.66), calls=%async_computation.1 | async-start | bytes 2097152 | tf_op jit(solution)/shard_map/while/body/eval_jaxpr/all_to_all | solution.py:56
  596.7 5.1 collective-permute-start.1
  611.9 33.3 %all-to-all-start.1 = ((bf16[32,2,4,2048]{3,2,1,0:T(4,128)(2,1)}), bf16[32,2,4,2048]{3,2,1,0:T(4,128)(2,1)S(1)}, u32[]{:S(2)}, u32[]{:S(2)}) async-start(bf16[32,2,4,2048]{3,2,1,0:T(4,128)(2,1)} %copy.66), calls=%async_computation.1 | async-start | bytes 2097152 | tf_op jit(solution)/shard_map/while/body/eval_jaxpr/all_to_all | solution.py:56
  645.8 5.1 collective-permute-start.1
  659.4 36.3 %copy-start.1 = (f32[5,32,4,64]{3,1,2,0:T(8,128)S(1)}, f32[5,32,4,64]{3,1,2,0:T(8,128)}, u32[]{:S(2)}) copy-start(f32[5,32,4,64]{3,1,2,0:T(8,128)} %copy-done) | copy-start | bytes 491524 | tf_op jit(solution)/shard_map/while
  660.9 34.1 %all-to-all-start.1 = ((bf16[32,2,4,2048]{3,2,1,0:T(4,128)(2,1)}), bf16[32,2,4,2048]{3,2,1,0:T(4,128)(2,1)S(1)}, u32[]{:S(2)}, u32[]{:S(2)}) async-start(bf16[32,2,4,2048]{3,2,1,0:T(4,128)(2,1)} %copy.66), calls=%async_computation.1 | async-start | bytes 2097152 | tf_op jit(solution)/shard_map/while/body/eval_jaxpr/all_to_all | solution.py:56
  695.7 5.1 collective-permute-start.1
  709.3 36.0 %copy-start.1 = (f32[5,32,4,64]{3,1,2,0:T(8,128)S(1)}, f32[5,32,4,64]{3,1,2,0:T(8,128)}, u32[]{:S(2)}) copy-start(f32[5,32,4,64]{3,1,2,0:T(8,128)} %copy-done) | copy-start | bytes 491524 | tf_op jit(solution)/shard_map/while
  710.8 33.9 %all-to-all-start.1 = ((bf16[32,2,4,2048]{3,2,1,0:T(4,128)(2,1)}), bf16[32,2,4,2048]{3,2,1,0:T(4,128)(2,1)S(1)}, u32[]{:S(2)}, u32[]{:S(2)}) async-start(bf16[32,2,4,2048]{3,2,1,0:T(4,128)(2,1)} %copy.66), calls=%async_computation.1 | async-start | bytes 2097152 | tf_op jit(solution)/shard_map/while/body/eval_jaxpr/all_to_all | solution.py:56
  745.3 5.1 collective-permute-start.1
  758.9 35.9 %copy-start.1 = (f32[5,32,4,64]{3,1,2,0:T(8,128)S(1)}, f32[5,32,4,64]{3,1,2,0:T(8,128)}, u32[]{:S(2)}) copy-start(f32[5,32,4,64]{3,1,2,0:T(8,128)} %copy-done) | copy-start | bytes 491524 | tf_op jit(solution)/shard_map/while
  760.5 33.8 %all-to-all-start.1 = ((bf16[32,2,4,2048]{3,2,1,0:T(4,128)(2,1)}), bf16[32,2,4,2048]{3,2,1,0:T(4,128)(2,1)S(1)}, u32[]{:S(2)}, u32[]{:S(2)}) async-start(bf16[32,2,4,2048]{3,2,1,0:T(4,128)(2,1)} %copy.66), calls=%async_computation.1 | async-start | bytes 2097152 | tf_op jit(solution)/shard_map/while/body/eval_jaxpr/all_to_all | solution.py:56
  794.8 5.1 collective-permute-start.1
  810.0 33.8 %all-to-all-start.1 = ((bf16[32,2,4,2048]{3,2,1,0:T(4,128)(2,1)}), bf16[32,2,4,2048]{3,2,1,0:T(4,128)(2,1)S(1)}, u32[]{:S(2)}, u32[]{:S(2)}) async-start(bf16[32,2,4,2048]{3,2,1,0:T(4,128)(2,1)} %copy.66), calls=%async_computation.1 | async-start | bytes 2097152 | tf_op jit(solution)/shard_map/while/body/eval_jaxpr/all_to_all | solution.py:56
  844.4 5.1 collective-permute-start.1
  859.5 33.8 %all-to-all-start.1 = ((bf16[32,2,4,2048]{3,2,1,0:T(4,128)(2,1)}), bf16[32,2,4,2048]{3,2,1,0:T(4,128)(2,1)S(1)}, u32[]{:S(2)}, u32[]{:S(2)}) async-start(bf16[32,2,4,2048]{3,2,1,0:T(4,128)(2,1)} %copy.66), calls=%async_computation.1 | async-start | bytes 2097152 | tf_op jit(solution)/shard_map/while/body/eval_jaxpr/all_to_all | solution.py:56
  893.9 5.1 collective-permute-start.1
  909.0 33.8 %all-to-all-start.1 = ((bf16[32,2,4,2048]{3,2,1,0:T(4,128)(2,1)}), bf16[32,2,4,2048]{3,2,1,0:T(4,128)(2,1)S(1)}, u32[]{:S(2)}, u32[]{:S(2)}) async-start(bf16[32,2,4,2048]{3,2,1,0:T(4,128)(2,1)} %copy.66), calls=%async_computation.1 | async-start | bytes 2097152 | tf_op jit(solution)/shard_map/while/body/eval_jaxpr/all_to_all | solution.py:56
  943.4 5.1 collective-permute-start.1
  958.5 33.8 %all-to-all-start.1 = ((bf16[32,2,4,2048]{3,2,1,0:T(4,128)(2,1)}), bf16[32,2,4,2048]{3,2,1,0:T(4,128)(2,1)S(1)}, u32[]{:S(2)}, u32[]{:S(2)}) async-start(bf16[32,2,4,2048]{3,2,1,0:T(4,128)(2,1)} %copy.66), calls=%async_computation.1 | async-start | bytes 2097152 | tf_op jit(solution)/shard_map/while/body/eval_jaxpr/all_to_all | solution.py:56
  992.9 5.1 collective-permute-start.1
  1008.0 33.8 %all-to-all-start.1 = ((bf16[32,2,4,2048]{3,2,1,0:T(4,128)(2,1)}), bf16[32,2,4,2048]{3,2,1,0:T(4,128)(2,1)S(1)}, u32[]{:S(2)}, u32[]{:S(2)}) async-start(bf16[32,2,4,2048]{3,2,1,0:T(4,128)(2,1)} %copy.66), calls=%async_computation.1 | async-start | bytes 2097152 | tf_op jit(solution)/shard_map/while/body/eval_jaxpr/all_to_all | solution.py:56
  1042.4 5.1 collective-permute-start.1
  1057.5 33.8 %all-to-all-start.1 = ((bf16[32,2,4,2048]{3,2,1,0:T(4,128)(2,1)}), bf16[32,2,4,2048]{3,2,1,0:T(4,128)(2,1)S(1)}, u32[]{:S(2)}, u32[]{:S(2)}) async-start(bf16[32,2,4,2048]{3,2,1,0:T(4,128)(2,1)} %copy.66), calls=%async_computation.1 | async-start | bytes 2097152 | tf_op jit(solution)/shard_map/while/body/eval_jaxpr/all_to_all | solution.py:56
  (20 other events, 353.2 us)
Sparse Core Ops, SparseCore 0:
  19.6 56.5 all-gather.3
where the time goes:
time: 1110 us
  waiting for transfers between devices  538 us (48%)
  starting transfers between devices  201 us (18%)
  local copies, waits for them, and re-layouts  137 us (12%)
  matrix products  120 us (11%)
  other arithmetic  81.5 us (7%)
  between operations  14.1 us (1%)
  blocking collectives  12.2 us (1%)
    all_to_all x11, waiting for transfers between devices, summed_on_arrival(): lax.all_to_all(in_blocks(value, dim, count), axis, 0, 0, tiled=True)  307 us
    all_to_all x11, waiting for transfers between devices, copy_for_each(): lax.all_to_all(jnp.broadcast_to(value[None], (count, *value.shape)), axis...  102 us
    ppermute x22, starting transfers between devices, passed_along(): lax.ppermute(value, axis, [(source, source + steps) for source in range(l...  97.6 us
    ppermute x22, waiting for transfers between devices, passed_along(): lax.ppermute(value, axis, [(source, source + steps) for source in range(l...  74.2 us
    all_to_all x11, starting transfers between devices, summed_on_arrival(): lax.all_to_all(in_blocks(value, dim, count), axis, 0, 0, tiled=True)  54.8 us
    all_gather x1, waiting for transfers between devices, all_blocks_2(): pieces = lax.all_gather(pieces, axes[k])  54.4 us
    all_to_all x11, starting transfers between devices, copy_for_each(): lax.all_to_all(jnp.broadcast_to(value[None], (count, *value.shape)), axis...  48.6 us
    dot_general x11, matrix products, backward_wave(): jnp.einsum('bjd,jkcd->jkbc', grad_pre, weight_blocks, preferred_element_t...  47.1 us
  transfers between devices with their start and end apart: 45, of which 44 were waited for; matrix products, arithmetic and copies ran while one was open for 7% of the time, Pallas kernels for 0%

commit v1 on v0

v1 whole, which is shorter than its diff:
```python
import jax
import jax.numpy as jnp
from jax import lax
from jax.experimental import pallas as pl
from jax.experimental.pallas import tpu as pltpu
from jax.sharding import Mesh
from jax.sharding import PartitionSpec as P

UNIT = ("unit_0", "unit_1")
STREAMS = 1
LANES = 128
SPARE = 4
F32 = jnp.float32
BF16 = jnp.bfloat16
VMEM = pl.BlockSpec(memory_space=pltpu.VMEM)
SMEM = pl.BlockSpec(memory_space=pltpu.SMEM)
ANY = pl.BlockSpec(memory_space=pl.ANY)


def dot(lhs, rhs, dims):
    return lax.dot_general(lhs, rhs, (dims, ((), ())), preferred_element_type=F32)


def local(value):
    return pltpu.with_memory_space_constraint(value, pltpu.VMEM)


def like(value):
    return jax.ShapeDtypeStruct(value.shape, value.dtype)


def forward_kernel(own, nnz, blk, half_chunks, copies, first_row):
    def body(
        layout_ref, meta_ref, src_ref, hid_ref, w_ref, bias_ref, extra_ref, cell_in, _b, _c, _d,
        cell_ref, picked_ref, fac_ref, hlog_ref, send_ref, w_s, picked_s, w_sems, out_sems,
    ):
        fetches = [
            pltpu.make_async_copy(w_ref.at[j], w_s.at[j], w_sems.at[j]) for j in range(own)
        ]
        for fetch in fetches:
            fetch.start()
        active = meta_ref[0] > 0
        slot = meta_ref[1]
        started = meta_ref[2] > 0
        rows = src_ref.shape[1]
        mine = slice(first_row, first_row + rows)
        upper = lax.broadcasted_iota(jnp.int32, (rows, LANES), 1) >= blk

        def block(j, index, half):
            number = layout_ref[j * nnz + index]
            chunk = number // 2
            value = jnp.where(
                chunk < half_chunks,
                src_ref[jnp.minimum(chunk, half_chunks - 1)],
                hid_ref[jnp.maximum(chunk - half_chunks, 0)],
            )
            return jnp.where(number % 2 == half, value, pltpu.roll(value, blk, 1))

        sums = []
        stores = []
        for j in range(own):
            pairs = [
                jnp.where(upper, block(j, 2 * k + 1, 1), block(j, 2 * k, 0)) for k in range(nnz // 2)
            ]
            picked = jnp.concatenate(pairs, 1)
            picked_s[j] = picked
            place = picked_ref.at[slot, j, pl.ds(first_row, rows)]
            stores.append(pltpu.make_async_copy(picked_s.at[j], place, out_sems.at[j]))
            stores[j].start()
            fetches[j].wait()
            sums.append(dot(picked, w_s[j], ((1,), (0,))) + bias_ref[j])
        pre_act = jnp.concatenate(sums, 0)
        gates = jax.nn.sigmoid(pre_act)
        update = jnp.tanh(pre_act[:, 2 * blk : 3 * blk])
        in_gate = gates[:, :blk]
        forget = gates[:, blk : 2 * blk]
        out_gate = gates[:, 3 * blk :]
        cell_prev = jnp.where(started, cell_in[...], 0.0)
        cell = forget * cell_prev + in_gate * update
        squash = jnp.tanh(cell)
        cell_ref[...] = cell
        hidden = jnp.where(active, out_gate * squash, 0.0).astype(BF16)
        front = [update * in_gate * (1.0 - in_gate), cell_prev * forget * (1.0 - forget)]
        second = [in_gate * (1.0 - update * update), squash * out_gate * (1.0 - out_gate)]
        third = [out_gate * (1.0 - squash * squash), forget]
        factors = jnp.concatenate(front + second + third, 1)
        chunks = []
        for j in range(own):
            for column in range(fac_ref.shape[0]):
                first = j * rows + column * fac_ref.shape[3]
                fac_ref[column, slot, j] = factors[first : first + fac_ref.shape[3]]
        for c in range(own // 2):
            lanes = slice(c * LANES, (c + 1) * LANES)
            low = hidden[2 * c * rows : (2 * c + 1) * rows]
            high = hidden[(2 * c + 1) * rows : (2 * c + 2) * rows]
            joined = jnp.concatenate([low, high], 1)
            hlog_ref[slot, mine, lanes] = joined
            chunks.append(joined + extra_ref[meta_ref[3], mine, lanes])
        payload = jnp.concatenate(chunks, 0)
        for d in range(copies):
            send_ref[d] = payload
        for store in stores:
            store.wait()

    return body


def forward_call(layout, meta, src, hid, w, bias, extra, cell, logs, copies, stream):
    own, wide, _ = w.shape
    half_chunks, rows, _ = src.shape
    nnz = layout.shape[0] // own
    blk = wide // nnz
    send = jax.ShapeDtypeStruct((copies, own // 2 * rows, LANES), BF16)
    return pl.pallas_call(
        forward_kernel(own, nnz, blk, half_chunks, copies, stream * rows),
        in_specs=[SMEM, SMEM, VMEM, VMEM, ANY, VMEM, VMEM, VMEM, ANY, VMEM, VMEM],
        out_specs=[VMEM, ANY, VMEM, VMEM, VMEM],
        out_shape=[like(cell), *map(like, logs), send],
        scratch_shapes=[
            pltpu.VMEM(w.shape, w.dtype),
            pltpu.VMEM((own, rows, wide), BF16),
            pltpu.SemaphoreType.DMA((own,)),
            pltpu.SemaphoreType.DMA((own,)),
        ],
        input_output_aliases={7: 0, 8: 1, 9: 2, 10: 3},
        name="forward_wave",
    )(layout, meta, local(src), local(hid), w, bias, extra, local(cell), logs[0], local(logs[1]), local(logs[2]))


def backward_kernel(own, nnz, blk, half_chunks, columns, rows):
    part_width = 512
    group = half_chunks // columns

    def body(layout_ref, meta_ref, above_ref, recur_ref, cot_ref, fac_ref, carry_in, _p, *rest):
        w_refs, (carry_ref, pre_ref, sent_ref, acc, grad_s, w_s, w_sems) = (
            rest[:columns],
            rest[columns:],
        )
        fetches = [
            [
                pltpu.make_async_copy(w_refs[d].at[j], w_s.at[d, j], w_sems.at[d, j])
                for j in range(own)
            ]
            for d in range(columns)
        ]
        for several in fetches:
            for fetch in several:
                fetch.start()
        active = meta_ref[0] > 0
        slot = meta_ref[1]
        step = meta_ref[3]
        upper = lax.broadcasted_iota(jnp.int32, (rows, LANES), 1) >= blk
        acc[...] = jnp.zeros_like(acc)
        spare = acc.shape[0]
        total = above_ref[...].astype(F32) + cot_ref[step].astype(F32)
        for d in range(recur_ref.shape[0]):
            total = total + recur_ref[d, 1].astype(F32)
        grads = []
        for c in range(columns * own // 2):
            piece = total[c * rows : (c + 1) * rows]
            grads += [piece[:, :blk], piece[:, blk:]]
        grad_hidden = jnp.concatenate(grads, 0)
        factors = fac_ref[:, step].reshape(columns * own * rows, 3 * LANES)
        grad_cell = carry_in[...] + grad_hidden * factors[:, 2 * LANES : 2 * LANES + blk]
        carry_ref[...] = jnp.where(active, grad_cell * factors[:, 2 * LANES + blk :], 0.0)
        spread = jnp.concatenate([grad_cell, grad_cell, grad_cell, grad_hidden], 1)
        grad_all = jnp.where(active, spread * factors[:, : 2 * LANES], 0.0)
        for column in range(columns):
            for j in range(own):
                first = (column * own + j) * rows
                piece = grad_all[first : first + rows]
                grad_s[column * own + j] = piece
                pre_ref[column, slot, j] = piece.astype(BF16)
        for d in range(columns):
            column = lax.rem(meta_ref[4] + (columns - d), columns)
            for j in range(own):
                grad_pre = grad_s[column * own + j].astype(BF16)
                fetches[d][j].wait()
                for part in range(nnz * blk // part_width):
                    rows_w = slice(part * part_width, (part + 1) * part_width)
                    contrib = dot(grad_pre, w_s[d, j, rows_w, :], ((1,), (1,)))
                    for q in range(part_width // LANES):
                        value = contrib[:, q * LANES : (q + 1) * LANES]
                        swapped = pltpu.roll(value, blk, 1)
                        for half in range(2):
                            place = part * (part_width // blk) + 2 * q + half
                            number = layout_ref[(d * own + j) * nnz + place]
                            odd = number % 2
                            placed = jnp.where(odd == half, value, swapped)
                            placed = jnp.where(upper == (odd == 1), placed, 0.0)
                            acc[(2 * q + half) % spare, number // 2] += placed
        width = own // 2
        for z in range(sent_ref.shape[0]):
            for side in range(2):
                for column in range(columns):
                    first = side * half_chunks + column * group + z * width
                    value = acc[0, first : first + width]
                    for extra in range(1, spare):
                        value = value + acc[extra, first : first + width]
                    value = value.reshape(width * rows, LANES)
                    lines = slice(column * width * rows, (column + 1) * width * rows)
                    sent_ref[z, side, lines] = value.astype(BF16)

    return body


def backward_call(layout, meta, above, recur, cot, w_all, fac, carry, pre):
    columns = len(w_all)
    own, wide, gate_width = w_all[0].shape
    rows = pre.shape[3]
    nnz = layout.shape[0] // (own * columns)
    blk = wide // nnz
    half_chunks = recur.shape[0] * columns * own // 2
    return pl.pallas_call(
        backward_kernel(own, nnz, blk, half_chunks, columns, rows),
        in_specs=[SMEM, SMEM] + [VMEM] * 6 + [ANY] * columns,
        out_specs=[VMEM] * 3,
        out_shape=[like(carry), like(pre), like(recur)],
        scratch_shapes=[
            pltpu.VMEM((SPARE, 2 * half_chunks, rows, LANES), F32),
            pltpu.VMEM((columns * own, rows, gate_width), F32),
            pltpu.VMEM((columns, own, wide, gate_width), BF16),
            pltpu.SemaphoreType.DMA((columns, own)),
        ],
        input_output_aliases={6: 0, 7: 1},
        name="backward_wave",
    )(layout, meta, local(above), local(recur), cot, fac, local(carry), local(pre), *w_all)


def total_kernel(parts_ref, out_ref):
    total = parts_ref[0, 0].astype(F32)
    for d in range(1, parts_ref.shape[0]):
        total = total + parts_ref[d, 0].astype(F32)
    out_ref[...] = total.astype(BF16)


def total_of(parts):
    return pl.pallas_call(
        total_kernel,
        in_specs=[VMEM],
        out_specs=VMEM,
        out_shape=jax.ShapeDtypeStruct(parts.shape[2:], BF16),
        name="arrival_sum",
    )(local(parts))


def weight_grad_kernel(picked_ref, pre_ref, grad_ref, bias_ref):
    steps, _, rows, wide = picked_ref.shape
    columns = pre_ref.shape[0]
    lhs = picked_ref[...].reshape(steps * rows, wide)
    pieces = [pre_ref[c, t, 0].astype(F32) for t in range(steps) for c in range(columns)]
    rhs = jnp.concatenate(pieces, 0)
    grad_ref[0] = dot(lhs, rhs.astype(BF16), ((0,), (0,))).astype(BF16)
    bias_ref[0] = jnp.sum(rhs, 0, keepdims=True)


def weight_grads(picked, pre, steps):
    _, own, rows, wide = picked.shape
    columns, _, _, few, gate_width = pre.shape
    return pl.pallas_call(
        weight_grad_kernel,
        grid=(own,),
        in_specs=[
            pl.BlockSpec((steps, 1, rows, wide), lambda j: (0, j, 0, 0)),
            pl.BlockSpec((columns, steps, 1, few, gate_width), lambda j: (0, 0, j, 0, 0)),
        ],
        out_specs=[
            pl.BlockSpec((1, wide, gate_width), lambda j: (j, 0, 0)),
            pl.BlockSpec((1, 1, gate_width), lambda j: (j, 0, 0)),
        ],
        out_shape=[
            jax.ShapeDtypeStruct((own, wide, gate_width), BF16),
            jax.ShapeDtypeStruct((own, 1, gate_width), F32),
        ],
        name="weight_grads",
    )(picked, pre)


def exchanged(pieces):
    return lax.all_to_all(pieces, UNIT, 0, 0, tiled=True)


def on_device(tokens, embed, weights, layout, bias, d_hidden):
    layer_count = lax.axis_size("layer")
    layer_idx = lax.axis_index("layer")
    devices = lax.axis_size(UNIT)
    columns = lax.axis_size("unit_0")
    steps, batch = tokens.shape
    vocab, unit_width = embed.shape
    own, nnz, blk, gate_width = weights.shape[1:]
    w = weights[0].reshape(own, nnz * blk, gate_width)
    lay = layout[0].reshape(-1)
    bias_rows = bias[0].reshape(own, 1, gate_width)
    waves = steps + layer_count - 1
    rows = batch // STREAMS
    chunks = devices * own // 2
    few = batch // columns
    lay_all = [lay]
    w_rows = w.reshape(own * nnz * blk, gate_width)
    piece_rows = -(-w_rows.shape[0] // (16 * waves)) * 16
    moves = {}
    for turn in range(1, columns):
        moves[turn] = [(c, (c + turn) % columns) for c in range(columns)]
        lay_all.append(lax.ppermute(lay, "unit_0", moves[turn]))
    lay_all = jnp.concatenate(lay_all, 0)
    cot = d_hidden[0].reshape(steps, columns, few, unit_width).transpose(1, 0, 2, 3)
    cot = lax.all_to_all(cot, "unit_0", 0, 0, tiled=True)
    cot = cot.reshape(columns, steps, few, own // 2, LANES).transpose(1, 0, 3, 2, 4)
    cot = cot.reshape(steps, columns * own // 2 * few, LANES)

    vocab_ids = jnp.arange(vocab, dtype=jnp.int32)
    onehot = (tokens.reshape(-1)[:, None] == vocab_ids[None, :]).astype(BF16)
    looked = dot(onehot, embed, ((1,), (0,))).astype(BF16).reshape(steps, batch, unit_width)
    is_last = layer_idx == layer_count - 1
    looked = jnp.where(is_last, looked, jnp.zeros_like(looked))
    extra = jnp.concatenate([looked, jnp.zeros((1, batch, unit_width), BF16)], 0)
    ring = [(src, (src + 1) % layer_count) for src in range(layer_count)]
    lower = [(src, src - 1) for src in range(1, layer_count)]

    def meta_of(time_step, extra_row):
        in_range = (time_step >= 0) & (time_step < steps)
        clipped = jnp.clip(time_step, 0, steps - 1)
        slot = jnp.where(in_range, time_step, steps)
        later = in_range & (time_step > 0)
        row = clipped if extra_row is None else extra_row
        place = jnp.arange(5, dtype=jnp.int32)
        late = jnp.where(place == 2, later.astype(jnp.int32), row)
        late = jnp.where(place == 4, lax.axis_index("unit_0"), late)
        early = jnp.where(place == 0, in_range.astype(jnp.int32), slot)
        return jnp.where(place < 2, early, late)

    def forward_meta(wave):
        return meta_of(wave - layer_idx, jnp.minimum(wave + 1, steps))

    def backward_meta(wave):
        return meta_of(steps - 1 - wave + (layer_count - 1 - layer_idx), None)

    def first_payload(s):
        mine = extra[0, s * rows : (s + 1) * rows]
        flat = mine.reshape(rows, own // 2, LANES).transpose(1, 0, 2).reshape(-1, LANES)
        return jnp.broadcast_to(flat[None], (devices, *flat.shape))

    def gather(payload):
        return exchanged(payload).reshape(chunks, rows, LANES)

    def step(stream, meta, below, here, cell, logs):
        cell, *logs, send = forward_call(
            lay, meta, below, here, w, bias_rows, extra, cell, logs, devices, stream
        )
        return cell, logs, send

    def forward_wave(wave, state):
        meta, ready, held, cells, logs, others = state
        cells = list(cells)
        first = jnp.minimum(wave * piece_rows, w_rows.shape[0] - piece_rows)
        piece = lax.dynamic_slice(w_rows, (first, 0), (piece_rows, gate_width))
        new_others = []
        for turn, other in zip(moves, others):
            moved = lax.ppermute(piece, "unit_0", moves[turn])
            new_others.append(lax.dynamic_update_slice(other, moved, (first, 0)))
        last = STREAMS - 1
        for s in range(STREAMS):
            stream = (last + s) % STREAMS
            below = lax.ppermute(ready, "layer", ring)
            if STREAMS > 1:
                arriving = gather(held)
            if s == 0:
                following = forward_meta(wave + 1)
            cells[stream], logs, send = step(stream, meta, below, ready, cells[stream], logs)
            if STREAMS == 1:
                arriving = gather(send)
            ready, held = arriving, send
        return following, ready, held, tuple(cells), tuple(logs), tuple(new_others)

    logs = (
        jnp.zeros((steps + 1, own, batch, nnz * blk), BF16),
        jnp.zeros((columns, steps + 1, own, few, 3 * LANES), F32),
        jnp.zeros((steps + 1, batch, unit_width), BF16),
    )
    cells = tuple(jnp.zeros((own * rows, blk), F32) for _ in range(STREAMS))
    others = tuple(jnp.zeros(w_rows.shape, BF16) for _ in moves)
    sent_first = first_payload(0)
    start = (forward_meta(0), gather(sent_first), sent_first, cells, logs, others)
    (picked, fac, hlog), others = lax.fori_loop(0, waves, forward_wave, start)[-2:]
    w_all = [w, *[other.reshape(w.shape) for other in others]]

    fac = lax.all_to_all(fac, "unit_0", 0, 0, tiled=True)

    def backward_wave(wave, state):
        meta, above, recur, carry, pre = state
        carry, pre, sent = backward_call(lay_all, meta, above, recur, cot, w_all, fac, carry, pre)
        recur = lax.all_to_all(sent, "unit_1", 0, 0, tiled=True)
        following = backward_meta(wave + 1)
        down = total_of(recur)
        above = lax.ppermute(down, "layer", lower)
        return following, above, recur, carry, pre

    lines = columns * own // 2 * few
    start = (
        backward_meta(0),
        jnp.zeros((lines, LANES), BF16),
        jnp.zeros((devices // columns, 2, lines, LANES), BF16),
        jnp.zeros((columns * own * few, blk), F32),
        jnp.zeros((columns, steps + 1, own, few, gate_width), BF16),
    )
    pre = lax.fori_loop(0, waves, backward_wave, start)[-1]
    pre = lax.all_to_all(pre, "unit_0", 0, 0, tiled=True)
    grad_w, grad_b = weight_grads(picked, pre, steps)
    return (
        hlog[:steps][None],
        grad_w.reshape(1, own, nnz, blk, gate_width),
        grad_b.reshape(1, own, gate_width),
    )


def solution(mesh):
    torus = Mesh(mesh.devices.reshape(mesh.shape["layer"], 4, 8), ("layer", "unit_0", "unit_1"))
    return jax.shard_map(
        on_device,
        mesh=torus,
        in_specs=(
            P(),
            P(None, UNIT),
            P("layer", UNIT, None, None, None),
            P("layer", UNIT, None),
            P("layer", UNIT, None),
            P("layer", None, None, UNIT),
        ),
        out_specs=(
            P("layer", None, None, UNIT),
            P("layer", UNIT, None, None, None),
            P("layer", UNIT, None),
        ),
        check_vma=False,
    )
```

time: 1110 us -> 1030 us (0.928)
  Pallas kernels: 0 us -> 201 us
  matrix products: 120 us -> 0.21 us
  waiting for transfers between devices: 538 us -> 421 us
  other arithmetic: 81.5 us -> 0.18 us
  starting transfers between devices: 201 us -> 276 us
  local copies, waits for them, and re-layouts: 137 us -> 123 us
  between operations: 14.1 us -> 0.76 us
  blocking collectives: 12.2 us -> 0 us
    all_to_all x22 -> x26, waiting for transfers between devices: 409 us -> 128 us  [the longest x11 104 us: backward_wave(): recur = lax.all_to_all(sent, 'unit_1', 0, 0, tiled=True)]
    ppermute x22 -> x58, waiting for transfers between devices: 74.2 us -> 294 us  [the longest x33 187 us: forward_wave(): moved = lax.ppermute(piece, 'unit_0', moves[turn])]
    pallas_call x0 -> x34, Pallas kernels: none -> 201 us  [the longest x11 122 us: backward_call(): pl.pallas_call(backward_kernel(own, nnz, blk, half_chunks, columns, rows)...]
    dot_general x34 -> x1, matrix products: 120 us -> 0.21 us  [dot(): lax.dot_general(lhs, rhs, (dims, ((), ())), preferred_element_type=F32)]
    dynamic_update_slice x11 -> x33, local copies, waits for them, and re-layouts: 0.09 us -> 91.6 us  [forward_wave(): new_others.append(lax.dynamic_update_slice(other, moved, (first, 0)))]
    all_to_all x22 -> x26, starting transfers between devices: 103 us -> 158 us  [the longest x12 93.9 us: exchanged(): return lax.all_to_all(pieces, UNIT, 0, 0, tiled=True)]
    all_gather x1 -> x0, waiting for transfers between devices: 54.4 us -> none  [all_blocks_2(): pieces = lax.all_gather(pieces, axes[k])]
    gather x24 -> x0, local copies, waits for them, and re-layouts: 31.2 us -> none  [the longest x22 22.1 us: forward_wave(): jnp.take(inputs, flat_layout, axis=0)]
  transfers between devices with their start and end apart: 45 -> 84, of which waited for: 44 -> 60; matrix products, arithmetic and copies ran while one was open for 7% -> 10% of each run, Pallas kernels for 0% -> 0%
where the time goes in v1:
time: 1030 us; the launch traced here: 1020 us
  waiting for transfers between devices  421 us (41%)
  starting transfers between devices  276 us (27%)
  Pallas kernels  201 us (20%)
  local copies, waits for them, and re-layouts  123 us (12%)
    ppermute x33, waiting for transfers between devices, forward_wave(): moved = lax.ppermute(piece, 'unit_0', moves[turn])  187 us
    pallas_call x11, Pallas kernels, backward_call(): pl.pallas_call(backward_kernel(own, nnz, blk, half_chunks, columns, rows)...  122 us
    all_to_all x11, waiting for transfers between devices, backward_wave(): recur = lax.all_to_all(sent, 'unit_1', 0, 0, tiled=True)  104 us
    all_to_all x12, starting transfers between devices, exchanged(): return lax.all_to_all(pieces, UNIT, 0, 0, tiled=True)  93.9 us
    dynamic_update_slice x33, local copies, waits for them, and re-layouts, forward_wave(): new_others.append(lax.dynamic_update_slice(other, moved, (first, 0)))  91.6 us
    pallas_call x11, Pallas kernels, forward_call(): pl.pallas_call(forward_kernel(own, nnz, blk, half_chunks, copies, stream...  67.8 us
    ppermute x11, waiting for transfers between devices, forward_wave(): below = lax.ppermute(ready, 'layer', ring)  67.4 us
    all_to_all x11, starting transfers between devices, backward_wave(): recur = lax.all_to_all(sent, 'unit_1', 0, 0, tiled=True)  53.4 us
  transfers between devices with their start and end apart: 84, of which 60 were waited for; matrix products, arithmetic and copies ran while one was open for 10% of the time, Pallas kernels for 0%

profile of v1, /device:TPU:41, one launch (start us, length us, event | category | flops | bytes accessed | tf_op | source)
XLA Modules:
  0.0 1023.1 jit_solution(12481344022304803182)
XLA Ops:
  12.5 8.9 all-to-all-start.2
  22.9 13.9 %all-to-all-done.2 = bf16[32,64,128]{2,1,0:T(8,128)(2,1)S(1)} async-done(((bf16[32,64,128]{2,1,0:T(8,128)(2,1)}), bf16[32,64,128]{2,1,0:T(8,128)(2,1)S(1)}, u32[]{:S(2)}, u32[]{:S(2)}) %all-to-all-start.2) | async-done | bytes 524320 | tf_op jit(solution)/shard_map/all_to_all | solution.py:280
  46.6 595.2 %while.54 = (s32[]{:T(128)}, s32[5]{0:T(128)S(1)}, bf16[64,32,128]{2,1,0:T(8,128)(2,1)S(1)}, f32[128,64]{1,0:T(8,128)S(1)}, bf16[5,4,32,2048]{3,2,1,0:T(8,128)(2...) while((s32[]{:T(128)}, s32[5]{0:T(128)S(1)}, ...), condition=%wide.region_1.2_spmd, body=%wide.region_0.1_spmd.sunk | while | flops 61 | bytes 11371147 | solution.py:384
  73.9 10.8 %collective-permute-done.1 = bf16[752,256]{1,0:T(8,128)(2,1)S(1)} collective-permute-done((bf16[752,256]{1,0:T(8,128)(2,1)S(1)}, bf16[752,256]{1,0:T(8,128)(2,1)S(1)}, u32[]{:S(2)}, u32[]{:S(2)}) %collective-permute-start.1) | collective-permute-done | bytes 385056 | tf_op jit(solution)/shard_map/while/body/eval_jaxpr/ppermute | solution.py:359
  114.4 7.9 all-to-all-start
  128.3 10.8 %collective-permute-done.1 = bf16[752,256]{1,0:T(8,128)(2,1)S(1)} collective-permute-done((bf16[752,256]{1,0:T(8,128)(2,1)S(1)}, bf16[752,256]{1,0:T(8,128)(2,1)S(1)}, u32[]{:S(2)}, u32[]{:S(2)}) %collective-permute-start.1) | collective-permute-done | bytes 385056 | tf_op jit(solution)/shard_map/while/body/eval_jaxpr/ppermute | solution.py:359
  167.0 7.2 all-to-all-start
  180.2 8.3 collective-permute-done.1
  191.2 7.6 collective-permute-done.2
  221.2 9.2 all-to-all-start
  236.4 11.0 %collective-permute-done.1 = bf16[752,256]{1,0:T(8,128)(2,1)S(1)} collective-permute-done((bf16[752,256]{1,0:T(8,128)(2,1)S(1)}, bf16[752,256]{1,0:T(8,128)(2,1)S(1)}, u32[]{:S(2)}, u32[]{:S(2)}) %collective-permute-start.1) | collective-permute-done | bytes 385056 | tf_op jit(solution)/shard_map/while/body/eval_jaxpr/ppermute | solution.py:359
  289.0 9.4 collective-permute-done.1
  330.1 9.2 all-to-all-start
  345.2 12.1 %collective-permute-done.1 = bf16[752,256]{1,0:T(8,128)(2,1)S(1)} collective-permute-done((bf16[752,256]{1,0:T(8,128)(2,1)S(1)}, bf16[752,256]{1,0:T(8,128)(2,1)S(1)}, u32[]{:S(2)}, u32[]{:S(2)}) %collective-permute-start.1) | collective-permute-done | bytes 385056 | tf_op jit(solution)/shard_map/while/body/eval_jaxpr/ppermute | solution.py:359
  384.1 8.9 all-to-all-start
  399.0 9.4 collective-permute-done.1
  438.7 7.2 all-to-all-start
  451.8 9.5 collective-permute-done.1
  490.8 7.2 all-to-all-start
  504.0 9.3 collective-permute-done.1
  545.0 9.2 all-to-all-start
  560.2 12.1 %collective-permute-done.1 = bf16[752,256]{1,0:T(8,128)(2,1)S(1)} collective-permute-done((bf16[752,256]{1,0:T(8,128)(2,1)S(1)}, bf16[752,256]{1,0:T(8,128)(2,1)S(1)}, u32[]{:S(2)}, u32[]{:S(2)}) %collective-permute-start.1) | collective-permute-done | bytes 385056 | tf_op jit(solution)/shard_map/while/body/eval_jaxpr/ppermute | solution.py:359
  602.6 7.8 all-to-all-start
  616.3 11.8 %collective-permute-done.1 = bf16[752,256]{1,0:T(8,128)(2,1)S(1)} collective-permute-done((bf16[752,256]{1,0:T(8,128)(2,1)S(1)}, bf16[752,256]{1,0:T(8,128)(2,1)S(1)}, u32[]{:S(2)}, u32[]{:S(2)}) %collective-permute-start.1) | collective-permute-done | bytes 385056 | tf_op jit(solution)/shard_map/while/body/eval_jaxpr/ppermute | solution.py:359
  660.9 345.9 %while.55 = (s32[]{:T(128)}, s32[5]{0:T(128)S(1)}, bf16[64,128]{1,0:T(8,128)(2,1)S(1)}, bf16[8,2,64,128]{3,2,1,0:T(8,128)(2,1)S(1)}, f32[128,64]{1,0:T(8,128)S(1...) while((s32[]{:T(128)}, s32[5]{0:T(128)S(1)}, ...), condition=%wide.region_3.4_spmd, body=%wide.region_2.3_spmd.sunk | while | flops 57 | bytes 852389 | solution.py:406
  660.9 11.2 %backward_wave.7 = (f32[128,64]{1,0:T(8,128)S(1)}, bf16[4,5,4,8,256]{4,3,2,1,0:T(8,128)(2,1)}, bf16[8,2,64,128]{3,2,1,0:T(8,128)(2,1)}) custom-call(s32[512]{0:T(512)S(1)} %get-tuple-element.1078.layout_ref, s32[5]{0:T(128)S(1)} %get-tuple-element.1053.meta_ref, ...), custom_call_target="tpu_custom_call", output_to_operand_aliasing={{0}: (6, {}), {1}: (7, {})} | custom-call | tf_op jit(solution)/shard_map/while/body/eval_jaxpr/backward_wave/pallas_call | solution.py:214
  672.2 7.2 all-to-all-start.1
  679.4 7.9 all-to-all-done.1.parts_ref
  694.6 11.1 %backward_wave.7 = (f32[128,64]{1,0:T(8,128)S(1)}, bf16[4,5,4,8,256]{4,3,2,1,0:T(8,128)(2,1)}, bf16[8,2,64,128]{3,2,1,0:T(8,128)(2,1)}) custom-call(s32[512]{0:T(512)S(1)} %get-tuple-element.1078.layout_ref, s32[5]{0:T(128)S(1)} %get-tuple-element.1053.meta_ref, ...), custom_call_target="tpu_custom_call", output_to_operand_aliasing={{0}: (6, {}), {1}: (7, {})} | custom-call | tf_op jit(solution)/shard_map/while/body/eval_jaxpr/backward_wave/pallas_call | solution.py:214
  710.1 8.6 all-to-all-done.1.parts_ref
  725.4 11.1 %backward_wave.7 = (f32[128,64]{1,0:T(8,128)S(1)}, bf16[4,5,4,8,256]{4,3,2,1,0:T(8,128)(2,1)}, bf16[8,2,64,128]{3,2,1,0:T(8,128)(2,1)}) custom-call(s32[512]{0:T(512)S(1)} %get-tuple-element.1078.layout_ref, s32[5]{0:T(128)S(1)} %get-tuple-element.1053.meta_ref, ...), custom_call_target="tpu_custom_call", output_to_operand_aliasing={{0}: (6, {}), {1}: (7, {})} | custom-call | tf_op jit(solution)/shard_map/while/body/eval_jaxpr/backward_wave/pallas_call | solution.py:214
  741.7 10.6 %all-to-all-done.1.parts_ref = bf16[8,2,64,128]{3,2,1,0:T(8,128)(2,1)S(1)} async-done(((bf16[8,2,64,128]{3,2,1,0:T(8,128)(2,1)}), bf16[8,2,64,128]{3,2,1,0:T(8,128)(2,1)S(1)}, u32[]{:S(2)}, u32[]{:S(2)}) %all-to-all-start.1) | async-done | bytes 262176 | tf_op jit(solution)/shard_map/while/body/eval_jaxpr/all_to_all | solution.py:392
  758.2 11.1 %backward_wave.7 = (f32[128,64]{1,0:T(8,128)S(1)}, bf16[4,5,4,8,256]{4,3,2,1,0:T(8,128)(2,1)}, bf16[8,2,64,128]{3,2,1,0:T(8,128)(2,1)}) custom-call(s32[512]{0:T(512)S(1)} %get-tuple-element.1078.layout_ref, s32[5]{0:T(128)S(1)} %get-tuple-element.1053.meta_ref, ...), custom_call_target="tpu_custom_call", output_to_operand_aliasing={{0}: (6, {}), {1}: (7, {})} | custom-call | tf_op jit(solution)/shard_map/while/body/eval_jaxpr/backward_wave/pallas_call | solution.py:214
  774.4 10.2 all-to-all-done.1.parts_ref
  790.4 11.1 %backward_wave.7 = (f32[128,64]{1,0:T(8,128)S(1)}, bf16[4,5,4,8,256]{4,3,2,1,0:T(8,128)(2,1)}, bf16[8,2,64,128]{3,2,1,0:T(8,128)(2,1)}) custom-call(s32[512]{0:T(512)S(1)} %get-tuple-element.1078.layout_ref, s32[5]{0:T(128)S(1)} %get-tuple-element.1053.meta_ref, ...), custom_call_target="tpu_custom_call", output_to_operand_aliasing={{0}: (6, {}), {1}: (7, {})} | custom-call | tf_op jit(solution)/shard_map/while/body/eval_jaxpr/backward_wave/pallas_call | solution.py:214
  806.0 9.5 all-to-all-done.1.parts_ref
  821.3 11.1 %backward_wave.7 = (f32[128,64]{1,0:T(8,128)S(1)}, bf16[4,5,4,8,256]{4,3,2,1,0:T(8,128)(2,1)}, bf16[8,2,64,128]{3,2,1,0:T(8,128)(2,1)}) custom-call(s32[512]{0:T(512)S(1)} %get-tuple-element.1078.layout_ref, s32[5]{0:T(128)S(1)} %get-tuple-element.1053.meta_ref, ...), custom_call_target="tpu_custom_call", output_to_operand_aliasing={{0}: (6, {}), {1}: (7, {})} | custom-call | tf_op jit(solution)/shard_map/while/body/eval_jaxpr/backward_wave/pallas_call | solution.py:214
  836.9 9.5 all-to-all-done.1.parts_ref
  852.3 11.1 %backward_wave.7 = (f32[128,64]{1,0:T(8,128)S(1)}, bf16[4,5,4,8,256]{4,3,2,1,0:T(8,128)(2,1)}, bf16[8,2,64,128]{3,2,1,0:T(8,128)(2,1)}) custom-call(s32[512]{0:T(512)S(1)} %get-tuple-element.1078.layout_ref, s32[5]{0:T(128)S(1)} %get-tuple-element.1053.meta_ref, ...), custom_call_target="tpu_custom_call", output_to_operand_aliasing={{0}: (6, {}), {1}: (7, {})} | custom-call | tf_op jit(solution)/shard_map/while/body/eval_jaxpr/backward_wave/pallas_call | solution.py:214
  867.8 9.5 all-to-all-done.1.parts_ref
  883.2 11.1 %backward_wave.7 = (f32[128,64]{1,0:T(8,128)S(1)}, bf16[4,5,4,8,256]{4,3,2,1,0:T(8,128)(2,1)}, bf16[8,2,64,128]{3,2,1,0:T(8,128)(2,1)}) custom-call(s32[512]{0:T(512)S(1)} %get-tuple-element.1078.layout_ref, s32[5]{0:T(128)S(1)} %get-tuple-element.1053.meta_ref, ...), custom_call_target="tpu_custom_call", output_to_operand_aliasing={{0}: (6, {}), {1}: (7, {})} | custom-call | tf_op jit(solution)/shard_map/while/body/eval_jaxpr/backward_wave/pallas_call | solution.py:214
  898.7 9.5 all-to-all-done.1.parts_ref
  914.1 11.1 %backward_wave.7 = (f32[128,64]{1,0:T(8,128)S(1)}, bf16[4,5,4,8,256]{4,3,2,1,0:T(8,128)(2,1)}, bf16[8,2,64,128]{3,2,1,0:T(8,128)(2,1)}) custom-call(s32[512]{0:T(512)S(1)} %get-tuple-element.1078.layout_ref, s32[5]{0:T(128)S(1)} %get-tuple-element.1053.meta_ref, ...), custom_call_target="tpu_custom_call", output_to_operand_aliasing={{0}: (6, {}), {1}: (7, {})} | custom-call | tf_op jit(solution)/shard_map/while/body/eval_jaxpr/backward_wave/pallas_call | solution.py:214
  929.7 9.5 all-to-all-done.1.parts_ref
  945.0 11.1 %backward_wave.7 = (f32[128,64]{1,0:T(8,128)S(1)}, bf16[4,5,4,8,256]{4,3,2,1,0:T(8,128)(2,1)}, bf16[8,2,64,128]{3,2,1,0:T(8,128)(2,1)}) custom-call(s32[512]{0:T(512)S(1)} %get-tuple-element.1078.layout_ref, s32[5]{0:T(128)S(1)} %get-tuple-element.1053.meta_ref, ...), custom_call_target="tpu_custom_call", output_to_operand_aliasing={{0}: (6, {}), {1}: (7, {})} | custom-call | tf_op jit(solution)/shard_map/while/body/eval_jaxpr/backward_wave/pallas_call | solution.py:214
  960.6 9.5 all-to-all-done.1.parts_ref
  976.0 11.1 %backward_wave.7 = (f32[128,64]{1,0:T(8,128)S(1)}, bf16[4,5,4,8,256]{4,3,2,1,0:T(8,128)(2,1)}, bf16[8,2,64,128]{3,2,1,0:T(8,128)(2,1)}) custom-call(s32[512]{0:T(512)S(1)} %get-tuple-element.1078.layout_ref, s32[5]{0:T(128)S(1)} %get-tuple-element.1053.meta_ref, ...), custom_call_target="tpu_custom_call", output_to_operand_aliasing={{0}: (6, {}), {1}: (7, {})} | custom-call | tf_op jit(solution)/shard_map/while/body/eval_jaxpr/backward_wave/pallas_call | solution.py:214
  991.5 9.5 all-to-all-done.1.parts_ref
  (255 shorter events, 570.2 us)
Async XLA Ops:
  12.5 24.3 %all-to-all-start.2 = ((bf16[32,64,128]{2,1,0:T(8,128)(2,1)}), bf16[32,64,128]{2,1,0:T(8,128)(2,1)S(1)}, u32[]{:S(2)}, u32[]{:S(2)}) async-start(bf16[32,64,128]{2,1,0:T(8,128)(2,1)} %broadcast_in_dim.168), calls=%async_computation.2 | async-start | bytes 1048576 | tf_op jit(solution)/shard_map/all_to_all | solution.py:280
  63.6 36.1 %all-to-all-start = ((bf16[32,64,128]{2,1,0:T(8,128)(2,1)}), bf16[32,64,128]{2,1,0:T(8,128)(2,1)S(1)}, u32[]{:S(2)}, u32[]{:S(2)}) async-start(bf16[32,64,128]{2,1,0:T(8,128)(2,1)} %get-tuple-element.939), calls=%async_computation | async-start | bytes 1048576 | tf_op jit(solution)/shard_map/while/body/eval_jaxpr/all_to_all | solution.py:280
  69.0 15.7 %collective-permute-start.1 = (bf16[752,256]{1,0:T(8,128)(2,1)S(1)}, bf16[752,256]{1,0:T(8,128)(2,1)S(1)}, u32[]{:S(2)}, u32[]{:S(2)}) collective-permute-start(bf16[752,256]{1,0:T(8,128)(2,1)S(1)} %constant_dynamic-slice_fusion.2), channel_id=1, source_target_pairs={{0,8},{8,16},{16,24},{24,0},{1,9},{9,17},{17,25},{25,1},{2,10},{10... | collective-permute-start | bytes 1155080 | tf_op jit(solution)/shard_map/while/body/eval_jaxpr/ppermute | solution.py:359
  70.3 23.8 %collective-permute-start.2 = (bf16[752,256]{1,0:T(8,128)(2,1)S(1)}, bf16[752,256]{1,0:T(8,128)(2,1)S(1)}, u32[]{:S(2)}, u32[]{:S(2)}) collective-permute-start(bf16[752,256]{1,0:T(8,128)(2,1)S(1)} %constant_dynamic-slice_fusion.2), channel_id=1, source_target_pairs={{0,16},{8,24},{16,0},{24,8},{1,17},{9,25},{17,1},{25,9},{2,18},{10... | collective-permute-start | bytes 1155080 | tf_op jit(solution)/shard_map/while/body/eval_jaxpr/ppermute | solution.py:359
  72.7 24.1 %collective-permute-start.3 = (bf16[752,256]{1,0:T(8,128)(2,1)S(1)}, bf16[752,256]{1,0:T(8,128)(2,1)S(1)}, u32[]{:S(2)}, u32[]{:S(2)}) collective-permute-start(bf16[752,256]{1,0:T(8,128)(2,1)S(1)} %constant_dynamic-slice_fusion.2), channel_id=1, source_target_pairs={{0,24},{8,0},{16,8},{24,16},{1,25},{9,1},{17,9},{25,17},{2,26},{10... | collective-permute-start | bytes 1155080 | tf_op jit(solution)/shard_map/while/body/eval_jaxpr/ppermute | solution.py:359
  114.4 39.6 %all-to-all-start = ((bf16[32,64,128]{2,1,0:T(8,128)(2,1)}), bf16[32,64,128]{2,1,0:T(8,128)(2,1)S(1)}, u32[]{:S(2)}, u32[]{:S(2)}) async-start(bf16[32,64,128]{2,1,0:T(8,128)(2,1)} %get-tuple-element.939), calls=%async_computation | async-start | bytes 1048576 | tf_op jit(solution)/shard_map/while/body/eval_jaxpr/all_to_all | solution.py:280
  123.4 15.7 %collective-permute-start.1 = (bf16[752,256]{1,0:T(8,128)(2,1)S(1)}, bf16[752,256]{1,0:T(8,128)(2,1)S(1)}, u32[]{:S(2)}, u32[]{:S(2)}) collective-permute-start(bf16[752,256]{1,0:T(8,128)(2,1)S(1)} %constant_dynamic-slice_fusion.2), channel_id=1, source_target_pairs={{0,8},{8,16},{16,24},{24,0},{1,9},{9,17},{17,25},{25,1},{2,10},{10... | collective-permute-start | bytes 1155080 | tf_op jit(solution)/shard_map/while/body/eval_jaxpr/ppermute | solution.py:359
  124.7 23.8 %collective-permute-start.2 = (bf16[752,256]{1,0:T(8,128)(2,1)S(1)}, bf16[752,256]{1,0:T(8,128)(2,1)S(1)}, u32[]{:S(2)}, u32[]{:S(2)}) collective-permute-start(bf16[752,256]{1,0:T(8,128)(2,1)S(1)} %constant_dynamic-slice_fusion.2), channel_id=1, source_target_pairs={{0,16},{8,24},{16,0},{24,8},{1,17},{9,25},{17,1},{25,9},{2,18},{10... | collective-permute-start | bytes 1155080 | tf_op jit(solution)/shard_map/while/body/eval_jaxpr/ppermute | solution.py:359
  127.1 24.1 %collective-permute-start.3 = (bf16[752,256]{1,0:T(8,128)(2,1)S(1)}, bf16[752,256]{1,0:T(8,128)(2,1)S(1)}, u32[]{:S(2)}, u32[]{:S(2)}) collective-permute-start(bf16[752,256]{1,0:T(8,128)(2,1)S(1)} %constant_dynamic-slice_fusion.2), channel_id=1, source_target_pairs={{0,24},{8,0},{16,8},{24,16},{1,25},{9,1},{17,9},{25,17},{2,26},{10... | collective-permute-start | bytes 1155080 | tf_op jit(solution)/shard_map/while/body/eval_jaxpr/ppermute | solution.py:359
  167.0 37.3 %all-to-all-start = ((bf16[32,64,128]{2,1,0:T(8,128)(2,1)}), bf16[32,64,128]{2,1,0:T(8,128)(2,1)S(1)}, u32[]{:S(2)}, u32[]{:S(2)}) async-start(bf16[32,64,128]{2,1,0:T(8,128)(2,1)} %get-tuple-element.939), calls=%async_computation | async-start | bytes 1048576 | tf_op jit(solution)/shard_map/while/body/eval_jaxpr/all_to_all | solution.py:280
  176.6 22.2 %collective-permute-start.2 = (bf16[752,256]{1,0:T(8,128)(2,1)S(1)}, bf16[752,256]{1,0:T(8,128)(2,1)S(1)}, u32[]{:S(2)}, u32[]{:S(2)}) collective-permute-start(bf16[752,256]{1,0:T(8,128)(2,1)S(1)} %constant_dynamic-slice_fusion.2), channel_id=1, source_target_pairs={{0,16},{8,24},{16,0},{24,8},{1,17},{9,25},{17,1},{25,9},{2,18},{10... | collective-permute-start | bytes 1155080 | tf_op jit(solution)/shard_map/while/body/eval_jaxpr/ppermute | solution.py:359
  179.0 22.6 %collective-permute-start.3 = (bf16[752,256]{1,0:T(8,128)(2,1)S(1)}, bf16[752,256]{1,0:T(8,128)(2,1)S(1)}, u32[]{:S(2)}, u32[]{:S(2)}) collective-permute-start(bf16[752,256]{1,0:T(8,128)(2,1)S(1)} %constant_dynamic-slice_fusion.2), channel_id=1, source_target_pairs={{0,24},{8,0},{16,8},{24,16},{1,25},{9,1},{17,9},{25,17},{2,26},{10... | collective-permute-start | bytes 1155080 | tf_op jit(solution)/shard_map/while/body/eval_jaxpr/ppermute | solution.py:359
  221.2 41.5 %all-to-all-start = ((bf16[32,64,128]{2,1,0:T(8,128)(2,1)}), bf16[32,64,128]{2,1,0:T(8,128)(2,1)S(1)}, u32[]{:S(2)}, u32[]{:S(2)}) async-start(bf16[32,64,128]{2,1,0:T(8,128)(2,1)} %get-tuple-element.939), calls=%async_computation | async-start | bytes 1048576 | tf_op jit(solution)/shard_map/while/body/eval_jaxpr/all_to_all | solution.py:280
  231.5 15.8 %collective-permute-start.1 = (bf16[752,256]{1,0:T(8,128)(2,1)S(1)}, bf16[752,256]{1,0:T(8,128)(2,1)S(1)}, u32[]{:S(2)}, u32[]{:S(2)}) collective-permute-start(bf16[752,256]{1,0:T(8,128)(2,1)S(1)} %constant_dynamic-slice_fusion.2), channel_id=1, source_target_pairs={{0,8},{8,16},{16,24},{24,0},{1,9},{9,17},{17,25},{25,1},{2,10},{10... | collective-permute-start | bytes 1155080 | tf_op jit(solution)/shard_map/while/body/eval_jaxpr/ppermute | solution.py:359
  232.8 24.4 %collective-permute-start.2 = (bf16[752,256]{1,0:T(8,128)(2,1)S(1)}, bf16[752,256]{1,0:T(8,128)(2,1)S(1)}, u32[]{:S(2)}, u32[]{:S(2)}) collective-permute-start(bf16[752,256]{1,0:T(8,128)(2,1)S(1)} %constant_dynamic-slice_fusion.2), channel_id=1, source_target_pairs={{0,16},{8,24},{16,0},{24,8},{1,17},{9,25},{17,1},{25,9},{2,18},{10... | collective-permute-start | bytes 1155080 | tf_op jit(solution)/shard_map/while/body/eval_jaxpr/ppermute | solution.py:359
  235.2 24.7 %collective-permute-start.3 = (bf16[752,256]{1,0:T(8,128)(2,1)S(1)}, bf16[752,256]{1,0:T(8,128)(2,1)S(1)}, u32[]{:S(2)}, u32[]{:S(2)}) collective-permute-start(bf16[752,256]{1,0:T(8,128)(2,1)S(1)} %constant_dynamic-slice_fusion.2), channel_id=1, source_target_pairs={{0,24},{8,0},{16,8},{24,16},{1,25},{9,1},{17,9},{25,17},{2,26},{10... | collective-permute-start | bytes 1155080 | tf_op jit(solution)/shard_map/while/body/eval_jaxpr/ppermute | solution.py:359
  275.9 37.7 %all-to-all-start = ((bf16[32,64,128]{2,1,0:T(8,128)(2,1)}), bf16[32,64,128]{2,1,0:T(8,128)(2,1)S(1)}, u32[]{:S(2)}, u32[]{:S(2)}) async-start(bf16[32,64,128]{2,1,0:T(8,128)(2,1)} %get-tuple-element.939), calls=%async_computation | async-start | bytes 1048576 | tf_op jit(solution)/shard_map/while/body/eval_jaxpr/all_to_all | solution.py:280
  284.1 14.3 %collective-permute-start.1 = (bf16[752,256]{1,0:T(8,128)(2,1)S(1)}, bf16[752,256]{1,0:T(8,128)(2,1)S(1)}, u32[]{:S(2)}, u32[]{:S(2)}) collective-permute-start(bf16[752,256]{1,0:T(8,128)(2,1)S(1)} %constant_dynamic-slice_fusion.2), channel_id=1, source_target_pairs={{0,8},{8,16},{16,24},{24,0},{1,9},{9,17},{17,25},{25,1},{2,10},{10... | collective-permute-start | bytes 1155080 | tf_op jit(solution)/shard_map/while/body/eval_jaxpr/ppermute | solution.py:359
  285.4 22.6 %collective-permute-start.2 = (bf16[752,256]{1,0:T(8,128)(2,1)S(1)}, bf16[752,256]{1,0:T(8,128)(2,1)S(1)}, u32[]{:S(2)}, u32[]{:S(2)}) collective-permute-start(bf16[752,256]{1,0:T(8,128)(2,1)S(1)} %constant_dynamic-slice_fusion.2), channel_id=1, source_target_pairs={{0,16},{8,24},{16,0},{24,8},{1,17},{9,25},{17,1},{25,9},{2,18},{10... | collective-permute-start | bytes 1155080 | tf_op jit(solution)/shard_map/while/body/eval_jaxpr/ppermute | solution.py:359
  287.9 22.9 %collective-permute-start.3 = (bf16[752,256]{1,0:T(8,128)(2,1)S(1)}, bf16[752,256]{1,0:T(8,128)(2,1)S(1)}, u32[]{:S(2)}, u32[]{:S(2)}) collective-permute-start(bf16[752,256]{1,0:T(8,128)(2,1)S(1)} %constant_dynamic-slice_fusion.2), channel_id=1, source_target_pairs={{0,24},{8,0},{16,8},{24,16},{1,25},{9,1},{17,9},{25,17},{2,26},{10... | collective-permute-start | bytes 1155080 | tf_op jit(solution)/shard_map/while/body/eval_jaxpr/ppermute | solution.py:359
  330.1 41.7 %all-to-all-start = ((bf16[32,64,128]{2,1,0:T(8,128)(2,1)}), bf16[32,64,128]{2,1,0:T(8,128)(2,1)S(1)}, u32[]{:S(2)}, u32[]{:S(2)}) async-start(bf16[32,64,128]{2,1,0:T(8,128)(2,1)} %get-tuple-element.939), calls=%async_computation | async-start | bytes 1048576 | tf_op jit(solution)/shard_map/while/body/eval_jaxpr/all_to_all | solution.py:280
  340.4 16.9 %collective-permute-start.1 = (bf16[752,256]{1,0:T(8,128)(2,1)S(1)}, bf16[752,256]{1,0:T(8,128)(2,1)S(1)}, u32[]{:S(2)}, u32[]{:S(2)}) collective-permute-start(bf16[752,256]{1,0:T(8,128)(2,1)S(1)} %constant_dynamic-slice_fusion.2), channel_id=1, source_target_pairs={{0,8},{8,16},{16,24},{24,0},{1,9},{9,17},{17,25},{25,1},{2,10},{10... | collective-permute-start | bytes 1155080 | tf_op jit(solution)/shard_map/while/body/eval_jaxpr/ppermute | solution.py:359
  341.6 24.6 %collective-permute-start.2 = (bf16[752,256]{1,0:T(8,128)(2,1)S(1)}, bf16[752,256]{1,0:T(8,128)(2,1)S(1)}, u32[]{:S(2)}, u32[]{:S(2)}) collective-permute-start(bf16[752,256]{1,0:T(8,128)(2,1)S(1)} %constant_dynamic-slice_fusion.2), channel_id=1, source_target_pairs={{0,16},{8,24},{16,0},{24,8},{1,17},{9,25},{17,1},{25,9},{2,18},{10... | collective-permute-start | bytes 1155080 | tf_op jit(solution)/shard_map/while/body/eval_jaxpr/ppermute | solution.py:359
  344.1 24.9 %collective-permute-start.3 = (bf16[752,256]{1,0:T(8,128)(2,1)S(1)}, bf16[752,256]{1,0:T(8,128)(2,1)S(1)}, u32[]{:S(2)}, u32[]{:S(2)}) collective-permute-start(bf16[752,256]{1,0:T(8,128)(2,1)S(1)} %constant_dynamic-slice_fusion.2), channel_id=1, source_target_pairs={{0,24},{8,0},{16,8},{24,16},{1,25},{9,1},{17,9},{25,17},{2,26},{10... | collective-permute-start | bytes 1155080 | tf_op jit(solution)/shard_map/while/body/eval_jaxpr/ppermute | solution.py:359
  384.1 39.4 %all-to-all-start = ((bf16[32,64,128]{2,1,0:T(8,128)(2,1)}), bf16[32,64,128]{2,1,0:T(8,128)(2,1)S(1)}, u32[]{:S(2)}, u32[]{:S(2)}) async-start(bf16[32,64,128]{2,1,0:T(8,128)(2,1)} %get-tuple-element.939), calls=%async_computation | async-start | bytes 1048576 | tf_op jit(solution)/shard_map/while/body/eval_jaxpr/all_to_all | solution.py:280
  394.1 14.3 %collective-permute-start.1 = (bf16[752,256]{1,0:T(8,128)(2,1)S(1)}, bf16[752,256]{1,0:T(8,128)(2,1)S(1)}, u32[]{:S(2)}, u32[]{:S(2)}) collective-permute-start(bf16[752,256]{1,0:T(8,128)(2,1)S(1)} %constant_dynamic-slice_fusion.2), channel_id=1, source_target_pairs={{0,8},{8,16},{16,24},{24,0},{1,9},{9,17},{17,25},{25,1},{2,10},{10... | collective-permute-start | bytes 1155080 | tf_op jit(solution)/shard_map/while/body/eval_jaxpr/ppermute | solution.py:359
  395.4 22.6 %collective-permute-start.2 = (bf16[752,256]{1,0:T(8,128)(2,1)S(1)}, bf16[752,256]{1,0:T(8,128)(2,1)S(1)}, u32[]{:S(2)}, u32[]{:S(2)}) collective-permute-start(bf16[752,256]{1,0:T(8,128)(2,1)S(1)} %constant_dynamic-slice_fusion.2), channel_id=1, source_target_pairs={{0,16},{8,24},{16,0},{24,8},{1,17},{9,25},{17,1},{25,9},{2,18},{10... | collective-permute-start | bytes 1155080 | tf_op jit(solution)/shard_map/while/body/eval_jaxpr/ppermute | solution.py:359
  397.8 22.9 %collective-permute-start.3 = (bf16[752,256]{1,0:T(8,128)(2,1)S(1)}, bf16[752,256]{1,0:T(8,128)(2,1)S(1)}, u32[]{:S(2)}, u32[]{:S(2)}) collective-permute-start(bf16[752,256]{1,0:T(8,128)(2,1)S(1)} %constant_dynamic-slice_fusion.2), channel_id=1, source_target_pairs={{0,24},{8,0},{16,8},{24,16},{1,25},{9,1},{17,9},{25,17},{2,26},{10... | collective-permute-start | bytes 1155080 | tf_op jit(solution)/shard_map/while/body/eval_jaxpr/ppermute | solution.py:359
  438.7 37.7 %all-to-all-start = ((bf16[32,64,128]{2,1,0:T(8,128)(2,1)}), bf16[32,64,128]{2,1,0:T(8,128)(2,1)S(1)}, u32[]{:S(2)}, u32[]{:S(2)}) async-start(bf16[32,64,128]{2,1,0:T(8,128)(2,1)} %get-tuple-element.939), calls=%async_computation | async-start | bytes 1048576 | tf_op jit(solution)/shard_map/while/body/eval_jaxpr/all_to_all | solution.py:280
  447.0 14.4 %collective-permute-start.1 = (bf16[752,256]{1,0:T(8,128)(2,1)S(1)}, bf16[752,256]{1,0:T(8,128)(2,1)S(1)}, u32[]{:S(2)}, u32[]{:S(2)}) collective-permute-start(bf16[752,256]{1,0:T(8,128)(2,1)S(1)} %constant_dynamic-slice_fusion.2), channel_id=1, source_target_pairs={{0,8},{8,16},{16,24},{24,0},{1,9},{9,17},{17,25},{25,1},{2,10},{10... | collective-permute-start | bytes 1155080 | tf_op jit(solution)/shard_map/while/body/eval_jaxpr/ppermute | solution.py:359
  448.3 22.6 %collective-permute-start.2 = (bf16[752,256]{1,0:T(8,128)(2,1)S(1)}, bf16[752,256]{1,0:T(8,128)(2,1)S(1)}, u32[]{:S(2)}, u32[]{:S(2)}) collective-permute-start(bf16[752,256]{1,0:T(8,128)(2,1)S(1)} %constant_dynamic-slice_fusion.2), channel_id=1, source_target_pairs={{0,16},{8,24},{16,0},{24,8},{1,17},{9,25},{17,1},{25,9},{2,18},{10... | collective-permute-start | bytes 1155080 | tf_op jit(solution)/shard_map/while/body/eval_jaxpr/ppermute | solution.py:359
  450.7 23.0 %collective-permute-start.3 = (bf16[752,256]{1,0:T(8,128)(2,1)S(1)}, bf16[752,256]{1,0:T(8,128)(2,1)S(1)}, u32[]{:S(2)}, u32[]{:S(2)}) collective-permute-start(bf16[752,256]{1,0:T(8,128)(2,1)S(1)} %constant_dynamic-slice_fusion.2), channel_id=1, source_target_pairs={{0,24},{8,0},{16,8},{24,16},{1,25},{9,1},{17,9},{25,17},{2,26},{10... | collective-permute-start | bytes 1155080 | tf_op jit(solution)/shard_map/while/body/eval_jaxpr/ppermute | solution.py:359
  490.8 37.6 %all-to-all-start = ((bf16[32,64,128]{2,1,0:T(8,128)(2,1)}), bf16[32,64,128]{2,1,0:T(8,128)(2,1)S(1)}, u32[]{:S(2)}, u32[]{:S(2)}) async-start(bf16[32,64,128]{2,1,0:T(8,128)(2,1)} %get-tuple-element.939), calls=%async_computation | async-start | bytes 1048576 | tf_op jit(solution)/shard_map/while/body/eval_jaxpr/all_to_all | solution.py:280
  499.1 14.2 %collective-permute-start.1 = (bf16[752,256]{1,0:T(8,128)(2,1)S(1)}, bf16[752,256]{1,0:T(8,128)(2,1)S(1)}, u32[]{:S(2)}, u32[]{:S(2)}) collective-permute-start(bf16[752,256]{1,0:T(8,128)(2,1)S(1)} %constant_dynamic-slice_fusion.2), channel_id=1, source_target_pairs={{0,8},{8,16},{16,24},{24,0},{1,9},{9,17},{17,25},{25,1},{2,10},{10... | collective-permute-start | bytes 1155080 | tf_op jit(solution)/shard_map/while/body/eval_jaxpr/ppermute | solution.py:359
  500.4 22.5 %collective-permute-start.2 = (bf16[752,256]{1,0:T(8,128)(2,1)S(1)}, bf16[752,256]{1,0:T(8,128)(2,1)S(1)}, u32[]{:S(2)}, u32[]{:S(2)}) collective-permute-start(bf16[752,256]{1,0:T(8,128)(2,1)S(1)} %constant_dynamic-slice_fusion.2), channel_id=1, source_target_pairs={{0,16},{8,24},{16,0},{24,8},{1,17},{9,25},{17,1},{25,9},{2,18},{10... | collective-permute-start | bytes 1155080 | tf_op jit(solution)/shard_map/while/body/eval_jaxpr/ppermute | solution.py:359
  502.8 22.8 %collective-permute-start.3 = (bf16[752,256]{1,0:T(8,128)(2,1)S(1)}, bf16[752,256]{1,0:T(8,128)(2,1)S(1)}, u32[]{:S(2)}, u32[]{:S(2)}) collective-permute-start(bf16[752,256]{1,0:T(8,128)(2,1)S(1)} %constant_dynamic-slice_fusion.2), channel_id=1, source_target_pairs={{0,24},{8,0},{16,8},{24,16},{1,25},{9,1},{17,9},{25,17},{2,26},{10... | collective-permute-start | bytes 1155080 | tf_op jit(solution)/shard_map/while/body/eval_jaxpr/ppermute | solution.py:359
  545.0 41.7 %all-to-all-start = ((bf16[32,64,128]{2,1,0:T(8,128)(2,1)}), bf16[32,64,128]{2,1,0:T(8,128)(2,1)S(1)}, u32[]{:S(2)}, u32[]{:S(2)}) async-start(bf16[32,64,128]{2,1,0:T(8,128)(2,1)} %get-tuple-element.939), calls=%async_computation | async-start | bytes 1048576 | tf_op jit(solution)/shard_map/while/body/eval_jaxpr/all_to_all | solution.py:280
  555.3 16.9 %collective-permute-start.1 = (bf16[752,256]{1,0:T(8,128)(2,1)S(1)}, bf16[752,256]{1,0:T(8,128)(2,1)S(1)}, u32[]{:S(2)}, u32[]{:S(2)}) collective-permute-start(bf16[752,256]{1,0:T(8,128)(2,1)S(1)} %constant_dynamic-slice_fusion.2), channel_id=1, source_target_pairs={{0,8},{8,16},{16,24},{24,0},{1,9},{9,17},{17,25},{25,1},{2,10},{10... | collective-permute-start | bytes 1155080 | tf_op jit(solution)/shard_map/while/body/eval_jaxpr/ppermute | solution.py:359
  556.6 24.5 %collective-permute-start.2 = (bf16[752,256]{1,0:T(8,128)(2,1)S(1)}, bf16[752,256]{1,0:T(8,128)(2,1)S(1)}, u32[]{:S(2)}, u32[]{:S(2)}) collective-permute-start(bf16[752,256]{1,0:T(8,128)(2,1)S(1)} %constant_dynamic-slice_fusion.2), channel_id=1, source_target_pairs={{0,16},{8,24},{16,0},{24,8},{1,17},{9,25},{17,1},{25,9},{2,18},{10... | collective-permute-start | bytes 1155080 | tf_op jit(solution)/shard_map/while/body/eval_jaxpr/ppermute | solution.py:359
  559.0 24.9 %collective-permute-start.3 = (bf16[752,256]{1,0:T(8,128)(2,1)S(1)}, bf16[752,256]{1,0:T(8,128)(2,1)S(1)}, u32[]{:S(2)}, u32[]{:S(2)}) collective-permute-start(bf16[752,256]{1,0:T(8,128)(2,1)S(1)} %constant_dynamic-slice_fusion.2), channel_id=1, source_target_pairs={{0,24},{8,0},{16,8},{24,16},{1,25},{9,1},{17,9},{25,17},{2,26},{10... | collective-permute-start | bytes 1155080 | tf_op jit(solution)/shard_map/while/body/eval_jaxpr/ppermute | solution.py:359
  602.6 39.3 %all-to-all-start = ((bf16[32,64,128]{2,1,0:T(8,128)(2,1)}), bf16[32,64,128]{2,1,0:T(8,128)(2,1)S(1)}, u32[]{:S(2)}, u32[]{:S(2)}) async-start(bf16[32,64,128]{2,1,0:T(8,128)(2,1)} %get-tuple-element.939), calls=%async_computation | async-start | bytes 1048576 | tf_op jit(solution)/shard_map/while/body/eval_jaxpr/all_to_all | solution.py:280
  611.4 16.6 %collective-permute-start.1 = (bf16[752,256]{1,0:T(8,128)(2,1)S(1)}, bf16[752,256]{1,0:T(8,128)(2,1)S(1)}, u32[]{:S(2)}, u32[]{:S(2)}) collective-permute-start(bf16[752,256]{1,0:T(8,128)(2,1)S(1)} %constant_dynamic-slice_fusion.2), channel_id=1, source_target_pairs={{0,8},{8,16},{16,24},{24,0},{1,9},{9,17},{17,25},{25,1},{2,10},{10... | collective-permute-start | bytes 1155080 | tf_op jit(solution)/shard_map/while/body/eval_jaxpr/ppermute | solution.py:359
  612.7 23.6 %collective-permute-start.2 = (bf16[752,256]{1,0:T(8,128)(2,1)S(1)}, bf16[752,256]{1,0:T(8,128)(2,1)S(1)}, u32[]{:S(2)}, u32[]{:S(2)}) collective-permute-start(bf16[752,256]{1,0:T(8,128)(2,1)S(1)} %constant_dynamic-slice_fusion.2), channel_id=1, source_target_pairs={{0,16},{8,24},{16,0},{24,8},{1,17},{9,25},{17,1},{25,9},{2,18},{10... | collective-permute-start | bytes 1155080 | tf_op jit(solution)/shard_map/while/body/eval_jaxpr/ppermute | solution.py:359
  615.1 24.0 %collective-permute-start.3 = (bf16[752,256]{1,0:T(8,128)(2,1)S(1)}, bf16[752,256]{1,0:T(8,128)(2,1)S(1)}, u32[]{:S(2)}, u32[]{:S(2)}) collective-permute-start(bf16[752,256]{1,0:T(8,128)(2,1)S(1)} %constant_dynamic-slice_fusion.2), channel_id=1, source_target_pairs={{0,24},{8,0},{16,8},{24,16},{1,25},{9,1},{17,9},{25,17},{2,26},{10... | collective-permute-start | bytes 1155080 | tf_op jit(solution)/shard_map/while/body/eval_jaxpr/ppermute | solution.py:359
  641.9 17.3 %all-to-all-start.4 = ((f32[4,5,4,8,384]{4,3,2,1,0:T(8,128)}), f32[4,5,4,8,384]{4,3,2,1,0:T(8,128)S(1)}, u32[]{:S(2)}, u32[]{:S(2)}) async-start(f32[4,5,4,8,384]{4,3,2,1,0:T(8,128)} %get-tuple-element.684), calls=%async_computation.4 | async-start | bytes 1966080 | tf_op jit(solution)/shard_map/all_to_all | solution.py:387
  672.2 15.1 %all-to-all-start.1 = ((bf16[8,2,64,128]{3,2,1,0:T(8,128)(2,1)}), bf16[8,2,64,128]{3,2,1,0:T(8,128)(2,1)S(1)}, u32[]{:S(2)}, u32[]{:S(2)}) async-start(bf16[8,2,64,128]{3,2,1,0:T(8,128)(2,1)} %get-tuple-element.958), calls=%async_computation.1 | async-start | bytes 524288 | tf_op jit(solution)/shard_map/while/body/eval_jaxpr/all_to_all | solution.py:392
  736.5 15.9 %all-to-all-start.1 = ((bf16[8,2,64,128]{3,2,1,0:T(8,128)(2,1)}), bf16[8,2,64,128]{3,2,1,0:T(8,128)(2,1)S(1)}, u32[]{:S(2)}, u32[]{:S(2)}) async-start(bf16[8,2,64,128]{3,2,1,0:T(8,128)(2,1)} %get-tuple-element.958), calls=%async_computation.1 | async-start | bytes 524288 | tf_op jit(solution)/shard_map/while/body/eval_jaxpr/all_to_all | solution.py:392
  769.3 15.3 %all-to-all-start.1 = ((bf16[8,2,64,128]{3,2,1,0:T(8,128)(2,1)}), bf16[8,2,64,128]{3,2,1,0:T(8,128)(2,1)S(1)}, u32[]{:S(2)}, u32[]{:S(2)}) async-start(bf16[8,2,64,128]{3,2,1,0:T(8,128)(2,1)} %get-tuple-element.958), calls=%async_computation.1 | async-start | bytes 524288 | tf_op jit(solution)/shard_map/while/body/eval_jaxpr/all_to_all | solution.py:392
  (40 other events, 690.6 us)

commit v2 on v1

--- a/solution.py
+++ b/solution.py
@@ -23,6 +23,15 @@
 
 def local(value):
     return pltpu.with_memory_space_constraint(value, pltpu.VMEM)
+
+
+def unset(*shapes):
+    return pl.pallas_call(
+        lambda *refs: None,
+        out_specs=[ANY] * len(shapes),
+        out_shape=[jax.ShapeDtypeStruct(shape, BF16) for shape in shapes],
+        name="unset",
+    )()
 
 
 def like(value):
@@ -85,10 +94,14 @@
         third = [out_gate * (1.0 - squash * squash), forget]
         factors = jnp.concatenate(front + second + third, 1)
         chunks = []
-        for j in range(own):
-            for column in range(fac_ref.shape[0]):
-                first = j * rows + column * fac_ref.shape[3]
-                fac_ref[column, slot, j] = factors[first : first + fac_ref.shape[3]]
+
+        @pl.when(active)
+        def _():
+            for j in range(own):
+                for column in range(fac_ref.shape[0]):
+                    first = j * rows + column * fac_ref.shape[3]
+                    fac_ref[column, slot, j] = factors[first : first + fac_ref.shape[3]]
+
         for c in range(own // 2):
             lanes = slice(c * LANES, (c + 1) * LANES)
             low = hidden[2 * c * rows : (2 * c + 1) * rows]
@@ -110,7 +123,7 @@
     half_chunks, rows, _ = src.shape
     nnz = layout.shape[0] // own
     blk = wide // nnz
-    send = jax.ShapeDtypeStruct((copies, own // 2 * rows, LANES), BF16)
+    send = pltpu.VMEM((copies, own // 2 * rows, LANES), BF16)
     return pl.pallas_call(
         forward_kernel(own, nnz, blk, half_chunks, copies, stream * rows),
         in_specs=[SMEM, SMEM, VMEM, VMEM, ANY, VMEM, VMEM, VMEM, ANY, VMEM, VMEM],
@@ -215,7 +228,7 @@
         backward_kernel(own, nnz, blk, half_chunks, columns, rows),
         in_specs=[SMEM, SMEM] + [VMEM] * 6 + [ANY] * columns,
         out_specs=[VMEM] * 3,
-        out_shape=[like(carry), like(pre), like(recur)],
+        out_shape=[like(carry), like(pre), pltpu.VMEM(recur.shape, recur.dtype)],
         scratch_shapes=[
             pltpu.VMEM((SPARE, 2 * half_chunks, rows, LANES), F32),
             pltpu.VMEM((columns * own, rows, gate_width), F32),
@@ -251,7 +264,7 @@
     pieces = [pre_ref[c, t, 0].astype(F32) for t in range(steps) for c in range(columns)]
     rhs = jnp.concatenate(pieces, 0)
     grad_ref[0] = dot(lhs, rhs.astype(BF16), ((0,), (0,))).astype(BF16)
-    bias_ref[0] = jnp.sum(rhs, 0, keepdims=True)
+    bias_ref[pl.ds(pl.program_id(0), 1)] = jnp.sum(rhs, 0, keepdims=True)
 
 
 def weight_grads(picked, pre, steps):
@@ -266,11 +279,11 @@
         ],
         out_specs=[
             pl.BlockSpec((1, wide, gate_width), lambda j: (j, 0, 0)),
-            pl.BlockSpec((1, 1, gate_width), lambda j: (j, 0, 0)),
+            pl.BlockSpec((own, gate_width), lambda j: (0, 0)),
         ],
         out_shape=[
             jax.ShapeDtypeStruct((own, wide, gate_width), BF16),
-            jax.ShapeDtypeStruct((own, 1, gate_width), F32),
+            jax.ShapeDtypeStruct((own, gate_width), F32),
         ],
         name="weight_grads",
     )(picked, pre)
@@ -372,15 +385,17 @@
             ready, held = arriving, send
         return following, ready, held, tuple(cells), tuple(logs), tuple(new_others)
 
+    picked, *others = unset(
+        (steps + 1, own, batch, nnz * blk), *[w_rows.shape for _ in moves]
+    )
     logs = (
-        jnp.zeros((steps + 1, own, batch, nnz * blk), BF16),
-        jnp.zeros((columns, steps + 1, own, few, 3 * LANES), F32),
+        picked,
+        jnp.zeros((columns, steps, own, few, 3 * LANES), F32),
         jnp.zeros((steps + 1, batch, unit_width), BF16),
     )
     cells = tuple(jnp.zeros((own * rows, blk), F32) for _ in range(STREAMS))
-    others = tuple(jnp.zeros(w_rows.shape, BF16) for _ in moves)
     sent_first = first_payload(0)
-    start = (forward_meta(0), gather(sent_first), sent_first, cells, logs, others)
+    start = (forward_meta(0), gather(sent_first), sent_first, cells, logs, tuple(others))
     (picked, fac, hlog), others = lax.fori_loop(0, waves, forward_wave, start)[-2:]
     w_all = [w, *[other.reshape(w.shape) for other in others]]
 

time: 1030 us -> 1010 us (0.981)
  local copies, waits for them, and re-layouts: 123 us -> 111 us
  transfers between devices with their start and end apart: 84 -> 84, of which waited for: 60 -> 60; matrix products, arithmetic and copies ran while one was open for 10% -> 11% of each run, Pallas kernels for 0% -> 0%
where the time goes in v2:
time: 1010 us; the launch traced here: 1000 us
  waiting for transfers between devices  422 us (42%)
  starting transfers between devices  268 us (27%)
  Pallas kernels  197 us (20%)
  local copies, waits for them, and re-layouts  111 us (11%)
    ppermute x33, waiting for transfers between devices, forward_wave(): moved = lax.ppermute(piece, 'unit_0', moves[turn])  185 us
    pallas_call x11, Pallas kernels, backward_call(): pl.pallas_call(backward_kernel(own, nnz, blk, half_chunks, columns, rows)...  118 us
    all_to_all x11, waiting for transfers between devices, backward_wave(): recur = lax.all_to_all(sent, 'unit_1', 0, 0, tiled=True)  105 us
    dynamic_update_slice x33, local copies, waits for them, and re-layouts, forward_wave(): new_others.append(lax.dynamic_update_slice(other, moved, (first, 0)))  91.6 us
    all_to_all x12, starting transfers between devices, exchanged(): return lax.all_to_all(pieces, UNIT, 0, 0, tiled=True)  89.1 us
    ppermute x11, waiting for transfers between devices, forward_wave(): below = lax.ppermute(ready, 'layer', ring)  67.4 us
    pallas_call x11, Pallas kernels, forward_call(): pl.pallas_call(forward_kernel(own, nnz, blk, half_chunks, copies, stream...  66.6 us
    all_to_all x11, starting transfers between devices, backward_wave(): recur = lax.all_to_all(sent, 'unit_1', 0, 0, tiled=True)  53.7 us
  transfers between devices with their start and end apart: 84, of which 60 were waited for; matrix products, arithmetic and copies ran while one was open for 11% of the time, Pallas kernels for 0%

profile of v2, /device:TPU:41, one launch (start us, length us, event | category | flops | bytes accessed | tf_op | source)
XLA Modules:
  0.0 1000.6 jit_solution(13849336202876663476)
XLA Ops:
  12.5 8.9 all-to-all-start.2
  23.0 13.9 %all-to-all-done.2 = bf16[32,64,128]{2,1,0:T(8,128)(2,1)S(1)} async-done(((bf16[32,64,128]{2,1,0:T(8,128)(2,1)}), bf16[32,64,128]{2,1,0:T(8,128)(2,1)S(1)}, u32[]{:S(2)}, u32[]{:S(2)}) %all-to-all-start.2) | async-done | bytes 524320 | tf_op jit(solution)/shard_map/all_to_all | solution.py:293
  37.8 587.6 %while.54 = (s32[]{:T(128)}, s32[5]{0:T(128)S(1)}, bf16[64,32,128]{2,1,0:T(8,128)(2,1)S(1)}, f32[128,64]{1,0:T(8,128)S(1)}, bf16[5,4,32,2048]{3,2,1,0:T(8,128)(2...) while((s32[]{:T(128)}, s32[5]{0:T(128)S(1)}, ...), condition=%wide.region_1.2_spmd, body=%wide.region_0.1_spmd.sunk | while | flops 61 | bytes 11371147 | solution.py:399
  64.9 10.8 %collective-permute-done.1 = bf16[752,256]{1,0:T(8,128)(2,1)S(1)} collective-permute-done((bf16[752,256]{1,0:T(8,128)(2,1)S(1)}, bf16[752,256]{1,0:T(8,128)(2,1)S(1)}, u32[]{:S(2)}, u32[]{:S(2)}) %collective-permute-start.1) | collective-permute-done | bytes 385056 | tf_op jit(solution)/shard_map/while/body/eval_jaxpr/ppermute | solution.py:372
  105.4 7.9 all-to-all-start
  119.2 10.8 %collective-permute-done.1 = bf16[752,256]{1,0:T(8,128)(2,1)S(1)} collective-permute-done((bf16[752,256]{1,0:T(8,128)(2,1)S(1)}, bf16[752,256]{1,0:T(8,128)(2,1)S(1)}, u32[]{:S(2)}, u32[]{:S(2)}) %collective-permute-start.1) | collective-permute-done | bytes 385056 | tf_op jit(solution)/shard_map/while/body/eval_jaxpr/ppermute | solution.py:372
  157.9 7.2 all-to-all-start
  171.0 8.3 collective-permute-done.1
  182.1 7.6 collective-permute-done.2
  212.0 9.2 all-to-all-start
  227.1 11.0 %collective-permute-done.1 = bf16[752,256]{1,0:T(8,128)(2,1)S(1)} collective-permute-done((bf16[752,256]{1,0:T(8,128)(2,1)S(1)}, bf16[752,256]{1,0:T(8,128)(2,1)S(1)}, u32[]{:S(2)}, u32[]{:S(2)}) %collective-permute-start.1) | collective-permute-done | bytes 385056 | tf_op jit(solution)/shard_map/while/body/eval_jaxpr/ppermute | solution.py:372
  266.5 7.2 all-to-all-start
  279.6 9.4 collective-permute-done.1
  333.5 10.9 %collective-permute-done.1 = bf16[752,256]{1,0:T(8,128)(2,1)S(1)} collective-permute-done((bf16[752,256]{1,0:T(8,128)(2,1)S(1)}, bf16[752,256]{1,0:T(8,128)(2,1)S(1)}, u32[]{:S(2)}, u32[]{:S(2)}) %collective-permute-start.1) | collective-permute-done | bytes 385056 | tf_op jit(solution)/shard_map/while/body/eval_jaxpr/ppermute | solution.py:372
  373.2 7.2 all-to-all-start
  386.3 9.5 collective-permute-done.1
  428.8 9.0 all-to-all-start
  443.8 11.5 %collective-permute-done.1 = bf16[752,256]{1,0:T(8,128)(2,1)S(1)} collective-permute-done((bf16[752,256]{1,0:T(8,128)(2,1)S(1)}, bf16[752,256]{1,0:T(8,128)(2,1)S(1)}, u32[]{:S(2)}, u32[]{:S(2)}) %collective-permute-start.1) | collective-permute-done | bytes 385056 | tf_op jit(solution)/shard_map/while/body/eval_jaxpr/ppermute | solution.py:372
  482.9 7.2 all-to-all-start
  496.0 11.4 %collective-permute-done.1 = bf16[752,256]{1,0:T(8,128)(2,1)S(1)} collective-permute-done((bf16[752,256]{1,0:T(8,128)(2,1)S(1)}, bf16[752,256]{1,0:T(8,128)(2,1)S(1)}, u32[]{:S(2)}, u32[]{:S(2)}) %collective-permute-start.1) | collective-permute-done | bytes 385056 | tf_op jit(solution)/shard_map/while/body/eval_jaxpr/ppermute | solution.py:372
  534.6 7.2 all-to-all-start
  547.8 8.5 collective-permute-done.1
  559.0 7.5 collective-permute-done.2
  600.8 9.5 collective-permute-done.1
  639.2 346.1 %while.55 = (s32[]{:T(128)}, s32[5]{0:T(128)S(1)}, bf16[64,128]{1,0:T(8,128)(2,1)S(1)}, bf16[8,2,64,128]{3,2,1,0:T(8,128)(2,1)S(1)}, f32[128,64]{1,0:T(8,128)S(1...) while((s32[]{:T(128)}, s32[5]{0:T(128)S(1)}, ...), condition=%wide.region_3.4_spmd, body=%wide.region_2.3_spmd.sunk | while | flops 57 | bytes 852389 | solution.py:421
  639.2 10.8 %backward_wave.7 = (f32[128,64]{1,0:T(8,128)S(1)}, bf16[4,5,4,8,256]{4,3,2,1,0:T(8,128)(2,1)}, bf16[8,2,64,128]{3,2,1,0:T(8,128)(2,1)}) custom-call(s32[512]{0:T(512)S(1)} %get-tuple-element.1074.layout_ref, s32[5]{0:T(128)S(1)} %get-tuple-element.1049.meta_ref, ...), custom_call_target="tpu_custom_call", output_to_operand_aliasing={{0}: (6, {}), {1}: (7, {})} | custom-call | tf_op jit(solution)/shard_map/while/body/eval_jaxpr/backward_wave/pallas_call | solution.py:227
  650.0 8.6 all-to-all-start.1
  658.6 8.2 all-to-all-done.1.parts_ref
  677.4 10.7 %backward_wave.7 = (f32[128,64]{1,0:T(8,128)S(1)}, bf16[4,5,4,8,256]{4,3,2,1,0:T(8,128)(2,1)}, bf16[8,2,64,128]{3,2,1,0:T(8,128)(2,1)}) custom-call(s32[512]{0:T(512)S(1)} %get-tuple-element.1074.layout_ref, s32[5]{0:T(128)S(1)} %get-tuple-element.1049.meta_ref, ...), custom_call_target="tpu_custom_call", output_to_operand_aliasing={{0}: (6, {}), {1}: (7, {})} | custom-call | tf_op jit(solution)/shard_map/while/body/eval_jaxpr/backward_wave/pallas_call | solution.py:227
  692.7 8.8 all-to-all-done.1.parts_ref
  707.4 10.7 %backward_wave.7 = (f32[128,64]{1,0:T(8,128)S(1)}, bf16[4,5,4,8,256]{4,3,2,1,0:T(8,128)(2,1)}, bf16[8,2,64,128]{3,2,1,0:T(8,128)(2,1)}) custom-call(s32[512]{0:T(512)S(1)} %get-tuple-element.1074.layout_ref, s32[5]{0:T(128)S(1)} %get-tuple-element.1049.meta_ref, ...), custom_call_target="tpu_custom_call", output_to_operand_aliasing={{0}: (6, {}), {1}: (7, {})} | custom-call | tf_op jit(solution)/shard_map/while/body/eval_jaxpr/backward_wave/pallas_call | solution.py:227
  722.6 11.1 %all-to-all-done.1.parts_ref = bf16[8,2,64,128]{3,2,1,0:T(8,128)(2,1)S(1)} async-done(((bf16[8,2,64,128]{3,2,1,0:T(8,128)(2,1)}), bf16[8,2,64,128]{3,2,1,0:T(8,128)(2,1)S(1)}, u32[]{:S(2)}, u32[]{:S(2)}) %all-to-all-start.1) | async-done | bytes 262176 | tf_op jit(solution)/shard_map/while/body/eval_jaxpr/all_to_all | solution.py:407
  739.6 10.7 %backward_wave.7 = (f32[128,64]{1,0:T(8,128)S(1)}, bf16[4,5,4,8,256]{4,3,2,1,0:T(8,128)(2,1)}, bf16[8,2,64,128]{3,2,1,0:T(8,128)(2,1)}) custom-call(s32[512]{0:T(512)S(1)} %get-tuple-element.1074.layout_ref, s32[5]{0:T(128)S(1)} %get-tuple-element.1049.meta_ref, ...), custom_call_target="tpu_custom_call", output_to_operand_aliasing={{0}: (6, {}), {1}: (7, {})} | custom-call | tf_op jit(solution)/shard_map/while/body/eval_jaxpr/backward_wave/pallas_call | solution.py:227
  755.0 10.2 %all-to-all-done.1.parts_ref = bf16[8,2,64,128]{3,2,1,0:T(8,128)(2,1)S(1)} async-done(((bf16[8,2,64,128]{3,2,1,0:T(8,128)(2,1)}), bf16[8,2,64,128]{3,2,1,0:T(8,128)(2,1)S(1)}, u32[]{:S(2)}, u32[]{:S(2)}) %all-to-all-start.1) | async-done | bytes 262176 | tf_op jit(solution)/shard_map/while/body/eval_jaxpr/all_to_all | solution.py:407
  771.0 10.7 %backward_wave.7 = (f32[128,64]{1,0:T(8,128)S(1)}, bf16[4,5,4,8,256]{4,3,2,1,0:T(8,128)(2,1)}, bf16[8,2,64,128]{3,2,1,0:T(8,128)(2,1)}) custom-call(s32[512]{0:T(512)S(1)} %get-tuple-element.1074.layout_ref, s32[5]{0:T(128)S(1)} %get-tuple-element.1049.meta_ref, ...), custom_call_target="tpu_custom_call", output_to_operand_aliasing={{0}: (6, {}), {1}: (7, {})} | custom-call | tf_op jit(solution)/shard_map/while/body/eval_jaxpr/backward_wave/pallas_call | solution.py:227
  786.3 9.5 all-to-all-done.1.parts_ref
  801.7 10.7 %backward_wave.7 = (f32[128,64]{1,0:T(8,128)S(1)}, bf16[4,5,4,8,256]{4,3,2,1,0:T(8,128)(2,1)}, bf16[8,2,64,128]{3,2,1,0:T(8,128)(2,1)}) custom-call(s32[512]{0:T(512)S(1)} %get-tuple-element.1074.layout_ref, s32[5]{0:T(128)S(1)} %get-tuple-element.1049.meta_ref, ...), custom_call_target="tpu_custom_call", output_to_operand_aliasing={{0}: (6, {}), {1}: (7, {})} | custom-call | tf_op jit(solution)/shard_map/while/body/eval_jaxpr/backward_wave/pallas_call | solution.py:227
  816.9 9.5 all-to-all-done.1.parts_ref
  832.3 10.7 %backward_wave.7 = (f32[128,64]{1,0:T(8,128)S(1)}, bf16[4,5,4,8,256]{4,3,2,1,0:T(8,128)(2,1)}, bf16[8,2,64,128]{3,2,1,0:T(8,128)(2,1)}) custom-call(s32[512]{0:T(512)S(1)} %get-tuple-element.1074.layout_ref, s32[5]{0:T(128)S(1)} %get-tuple-element.1049.meta_ref, ...), custom_call_target="tpu_custom_call", output_to_operand_aliasing={{0}: (6, {}), {1}: (7, {})} | custom-call | tf_op jit(solution)/shard_map/while/body/eval_jaxpr/backward_wave/pallas_call | solution.py:227
  847.5 9.5 all-to-all-done.1.parts_ref
  862.9 10.7 %backward_wave.7 = (f32[128,64]{1,0:T(8,128)S(1)}, bf16[4,5,4,8,256]{4,3,2,1,0:T(8,128)(2,1)}, bf16[8,2,64,128]{3,2,1,0:T(8,128)(2,1)}) custom-call(s32[512]{0:T(512)S(1)} %get-tuple-element.1074.layout_ref, s32[5]{0:T(128)S(1)} %get-tuple-element.1049.meta_ref, ...), custom_call_target="tpu_custom_call", output_to_operand_aliasing={{0}: (6, {}), {1}: (7, {})} | custom-call | tf_op jit(solution)/shard_map/while/body/eval_jaxpr/backward_wave/pallas_call | solution.py:227
  878.1 9.5 all-to-all-done.1.parts_ref
  893.5 10.7 %backward_wave.7 = (f32[128,64]{1,0:T(8,128)S(1)}, bf16[4,5,4,8,256]{4,3,2,1,0:T(8,128)(2,1)}, bf16[8,2,64,128]{3,2,1,0:T(8,128)(2,1)}) custom-call(s32[512]{0:T(512)S(1)} %get-tuple-element.1074.layout_ref, s32[5]{0:T(128)S(1)} %get-tuple-element.1049.meta_ref, ...), custom_call_target="tpu_custom_call", output_to_operand_aliasing={{0}: (6, {}), {1}: (7, {})} | custom-call | tf_op jit(solution)/shard_map/while/body/eval_jaxpr/backward_wave/pallas_call | solution.py:227
  908.7 9.5 all-to-all-done.1.parts_ref
  924.1 10.7 %backward_wave.7 = (f32[128,64]{1,0:T(8,128)S(1)}, bf16[4,5,4,8,256]{4,3,2,1,0:T(8,128)(2,1)}, bf16[8,2,64,128]{3,2,1,0:T(8,128)(2,1)}) custom-call(s32[512]{0:T(512)S(1)} %get-tuple-element.1074.layout_ref, s32[5]{0:T(128)S(1)} %get-tuple-element.1049.meta_ref, ...), custom_call_target="tpu_custom_call", output_to_operand_aliasing={{0}: (6, {}), {1}: (7, {})} | custom-call | tf_op jit(solution)/shard_map/while/body/eval_jaxpr/backward_wave/pallas_call | solution.py:227
  939.3 9.5 all-to-all-done.1.parts_ref
  954.7 10.7 %backward_wave.7 = (f32[128,64]{1,0:T(8,128)S(1)}, bf16[4,5,4,8,256]{4,3,2,1,0:T(8,128)(2,1)}, bf16[8,2,64,128]{3,2,1,0:T(8,128)(2,1)}) custom-call(s32[512]{0:T(512)S(1)} %get-tuple-element.1074.layout_ref, s32[5]{0:T(128)S(1)} %get-tuple-element.1049.meta_ref, ...), custom_call_target="tpu_custom_call", output_to_operand_aliasing={{0}: (6, {}), {1}: (7, {})} | custom-call | tf_op jit(solution)/shard_map/while/body/eval_jaxpr/backward_wave/pallas_call | solution.py:227
  970.0 9.5 all-to-all-done.1.parts_ref
  (247 shorter events, 556.3 us)
Async XLA Ops:
  12.5 24.3 %all-to-all-start.2 = ((bf16[32,64,128]{2,1,0:T(8,128)(2,1)}), bf16[32,64,128]{2,1,0:T(8,128)(2,1)S(1)}, u32[]{:S(2)}, u32[]{:S(2)}) async-start(bf16[32,64,128]{2,1,0:T(8,128)(2,1)} %broadcast_in_dim.165), calls=%async_computation.2 | async-start | bytes 1048576 | tf_op jit(solution)/shard_map/all_to_all | solution.py:293
  54.7 36.0 %all-to-all-start = ((bf16[32,64,128]{2,1,0:T(8,128)(2,1)}), bf16[32,64,128]{2,1,0:T(8,128)(2,1)S(1)}, u32[]{:S(2)}, u32[]{:S(2)}) async-start(bf16[32,64,128]{2,1,0:T(8,128)(2,1)} %get-tuple-element.935), calls=%async_computation | async-start | bytes 1048576 | tf_op jit(solution)/shard_map/while/body/eval_jaxpr/all_to_all | solution.py:293
  60.1 15.7 %collective-permute-start.1 = (bf16[752,256]{1,0:T(8,128)(2,1)S(1)}, bf16[752,256]{1,0:T(8,128)(2,1)S(1)}, u32[]{:S(2)}, u32[]{:S(2)}) collective-permute-start(bf16[752,256]{1,0:T(8,128)(2,1)S(1)} %constant_dynamic-slice_fusion.2), channel_id=1, source_target_pairs={{0,8},{8,16},{16,24},{24,0},{1,9},{9,17},{17,25},{25,1},{2,10},{10... | collective-permute-start | bytes 1155080 | tf_op jit(solution)/shard_map/while/body/eval_jaxpr/ppermute | solution.py:372
  61.4 23.8 %collective-permute-start.2 = (bf16[752,256]{1,0:T(8,128)(2,1)S(1)}, bf16[752,256]{1,0:T(8,128)(2,1)S(1)}, u32[]{:S(2)}, u32[]{:S(2)}) collective-permute-start(bf16[752,256]{1,0:T(8,128)(2,1)S(1)} %constant_dynamic-slice_fusion.2), channel_id=1, source_target_pairs={{0,16},{8,24},{16,0},{24,8},{1,17},{9,25},{17,1},{25,9},{2,18},{10... | collective-permute-start | bytes 1155080 | tf_op jit(solution)/shard_map/while/body/eval_jaxpr/ppermute | solution.py:372
  63.8 24.1 %collective-permute-start.3 = (bf16[752,256]{1,0:T(8,128)(2,1)S(1)}, bf16[752,256]{1,0:T(8,128)(2,1)S(1)}, u32[]{:S(2)}, u32[]{:S(2)}) collective-permute-start(bf16[752,256]{1,0:T(8,128)(2,1)S(1)} %constant_dynamic-slice_fusion.2), channel_id=1, source_target_pairs={{0,24},{8,0},{16,8},{24,16},{1,25},{9,1},{17,9},{25,17},{2,26},{10... | collective-permute-start | bytes 1155080 | tf_op jit(solution)/shard_map/while/body/eval_jaxpr/ppermute | solution.py:372
  105.4 39.6 %all-to-all-start = ((bf16[32,64,128]{2,1,0:T(8,128)(2,1)}), bf16[32,64,128]{2,1,0:T(8,128)(2,1)S(1)}, u32[]{:S(2)}, u32[]{:S(2)}) async-start(bf16[32,64,128]{2,1,0:T(8,128)(2,1)} %get-tuple-element.935), calls=%async_computation | async-start | bytes 1048576 | tf_op jit(solution)/shard_map/while/body/eval_jaxpr/all_to_all | solution.py:293
  114.4 15.7 %collective-permute-start.1 = (bf16[752,256]{1,0:T(8,128)(2,1)S(1)}, bf16[752,256]{1,0:T(8,128)(2,1)S(1)}, u32[]{:S(2)}, u32[]{:S(2)}) collective-permute-start(bf16[752,256]{1,0:T(8,128)(2,1)S(1)} %constant_dynamic-slice_fusion.2), channel_id=1, source_target_pairs={{0,8},{8,16},{16,24},{24,0},{1,9},{9,17},{17,25},{25,1},{2,10},{10... | collective-permute-start | bytes 1155080 | tf_op jit(solution)/shard_map/while/body/eval_jaxpr/ppermute | solution.py:372
  115.6 23.8 %collective-permute-start.2 = (bf16[752,256]{1,0:T(8,128)(2,1)S(1)}, bf16[752,256]{1,0:T(8,128)(2,1)S(1)}, u32[]{:S(2)}, u32[]{:S(2)}) collective-permute-start(bf16[752,256]{1,0:T(8,128)(2,1)S(1)} %constant_dynamic-slice_fusion.2), channel_id=1, source_target_pairs={{0,16},{8,24},{16,0},{24,8},{1,17},{9,25},{17,1},{25,9},{2,18},{10... | collective-permute-start | bytes 1155080 | tf_op jit(solution)/shard_map/while/body/eval_jaxpr/ppermute | solution.py:372
  118.1 24.1 %collective-permute-start.3 = (bf16[752,256]{1,0:T(8,128)(2,1)S(1)}, bf16[752,256]{1,0:T(8,128)(2,1)S(1)}, u32[]{:S(2)}, u32[]{:S(2)}) collective-permute-start(bf16[752,256]{1,0:T(8,128)(2,1)S(1)} %constant_dynamic-slice_fusion.2), channel_id=1, source_target_pairs={{0,24},{8,0},{16,8},{24,16},{1,25},{9,1},{17,9},{25,17},{2,26},{10... | collective-permute-start | bytes 1155080 | tf_op jit(solution)/shard_map/while/body/eval_jaxpr/ppermute | solution.py:372
  157.9 37.3 %all-to-all-start = ((bf16[32,64,128]{2,1,0:T(8,128)(2,1)}), bf16[32,64,128]{2,1,0:T(8,128)(2,1)S(1)}, u32[]{:S(2)}, u32[]{:S(2)}) async-start(bf16[32,64,128]{2,1,0:T(8,128)(2,1)} %get-tuple-element.935), calls=%async_computation | async-start | bytes 1048576 | tf_op jit(solution)/shard_map/while/body/eval_jaxpr/all_to_all | solution.py:293
  167.4 22.2 %collective-permute-start.2 = (bf16[752,256]{1,0:T(8,128)(2,1)S(1)}, bf16[752,256]{1,0:T(8,128)(2,1)S(1)}, u32[]{:S(2)}, u32[]{:S(2)}) collective-permute-start(bf16[752,256]{1,0:T(8,128)(2,1)S(1)} %constant_dynamic-slice_fusion.2), channel_id=1, source_target_pairs={{0,16},{8,24},{16,0},{24,8},{1,17},{9,25},{17,1},{25,9},{2,18},{10... | collective-permute-start | bytes 1155080 | tf_op jit(solution)/shard_map/while/body/eval_jaxpr/ppermute | solution.py:372
  169.9 22.5 %collective-permute-start.3 = (bf16[752,256]{1,0:T(8,128)(2,1)S(1)}, bf16[752,256]{1,0:T(8,128)(2,1)S(1)}, u32[]{:S(2)}, u32[]{:S(2)}) collective-permute-start(bf16[752,256]{1,0:T(8,128)(2,1)S(1)} %constant_dynamic-slice_fusion.2), channel_id=1, source_target_pairs={{0,24},{8,0},{16,8},{24,16},{1,25},{9,1},{17,9},{25,17},{2,26},{10... | collective-permute-start | bytes 1155080 | tf_op jit(solution)/shard_map/while/body/eval_jaxpr/ppermute | solution.py:372
  212.0 41.5 %all-to-all-start = ((bf16[32,64,128]{2,1,0:T(8,128)(2,1)}), bf16[32,64,128]{2,1,0:T(8,128)(2,1)S(1)}, u32[]{:S(2)}, u32[]{:S(2)}) async-start(bf16[32,64,128]{2,1,0:T(8,128)(2,1)} %get-tuple-element.935), calls=%async_computation | async-start | bytes 1048576 | tf_op jit(solution)/shard_map/while/body/eval_jaxpr/all_to_all | solution.py:293
  222.2 15.8 %collective-permute-start.1 = (bf16[752,256]{1,0:T(8,128)(2,1)S(1)}, bf16[752,256]{1,0:T(8,128)(2,1)S(1)}, u32[]{:S(2)}, u32[]{:S(2)}) collective-permute-start(bf16[752,256]{1,0:T(8,128)(2,1)S(1)} %constant_dynamic-slice_fusion.2), channel_id=1, source_target_pairs={{0,8},{8,16},{16,24},{24,0},{1,9},{9,17},{17,25},{25,1},{2,10},{10... | collective-permute-start | bytes 1155080 | tf_op jit(solution)/shard_map/while/body/eval_jaxpr/ppermute | solution.py:372
  223.5 24.4 %collective-permute-start.2 = (bf16[752,256]{1,0:T(8,128)(2,1)S(1)}, bf16[752,256]{1,0:T(8,128)(2,1)S(1)}, u32[]{:S(2)}, u32[]{:S(2)}) collective-permute-start(bf16[752,256]{1,0:T(8,128)(2,1)S(1)} %constant_dynamic-slice_fusion.2), channel_id=1, source_target_pairs={{0,16},{8,24},{16,0},{24,8},{1,17},{9,25},{17,1},{25,9},{2,18},{10... | collective-permute-start | bytes 1155080 | tf_op jit(solution)/shard_map/while/body/eval_jaxpr/ppermute | solution.py:372
  226.0 24.7 %collective-permute-start.3 = (bf16[752,256]{1,0:T(8,128)(2,1)S(1)}, bf16[752,256]{1,0:T(8,128)(2,1)S(1)}, u32[]{:S(2)}, u32[]{:S(2)}) collective-permute-start(bf16[752,256]{1,0:T(8,128)(2,1)S(1)} %constant_dynamic-slice_fusion.2), channel_id=1, source_target_pairs={{0,24},{8,0},{16,8},{24,16},{1,25},{9,1},{17,9},{25,17},{2,26},{10... | collective-permute-start | bytes 1155080 | tf_op jit(solution)/shard_map/while/body/eval_jaxpr/ppermute | solution.py:372
  266.5 37.7 %all-to-all-start = ((bf16[32,64,128]{2,1,0:T(8,128)(2,1)}), bf16[32,64,128]{2,1,0:T(8,128)(2,1)S(1)}, u32[]{:S(2)}, u32[]{:S(2)}) async-start(bf16[32,64,128]{2,1,0:T(8,128)(2,1)} %get-tuple-element.935), calls=%async_computation | async-start | bytes 1048576 | tf_op jit(solution)/shard_map/while/body/eval_jaxpr/all_to_all | solution.py:293
  274.8 14.3 %collective-permute-start.1 = (bf16[752,256]{1,0:T(8,128)(2,1)S(1)}, bf16[752,256]{1,0:T(8,128)(2,1)S(1)}, u32[]{:S(2)}, u32[]{:S(2)}) collective-permute-start(bf16[752,256]{1,0:T(8,128)(2,1)S(1)} %constant_dynamic-slice_fusion.2), channel_id=1, source_target_pairs={{0,8},{8,16},{16,24},{24,0},{1,9},{9,17},{17,25},{25,1},{2,10},{10... | collective-permute-start | bytes 1155080 | tf_op jit(solution)/shard_map/while/body/eval_jaxpr/ppermute | solution.py:372
  276.0 22.6 %collective-permute-start.2 = (bf16[752,256]{1,0:T(8,128)(2,1)S(1)}, bf16[752,256]{1,0:T(8,128)(2,1)S(1)}, u32[]{:S(2)}, u32[]{:S(2)}) collective-permute-start(bf16[752,256]{1,0:T(8,128)(2,1)S(1)} %constant_dynamic-slice_fusion.2), channel_id=1, source_target_pairs={{0,16},{8,24},{16,0},{24,8},{1,17},{9,25},{17,1},{25,9},{2,18},{10... | collective-permute-start | bytes 1155080 | tf_op jit(solution)/shard_map/while/body/eval_jaxpr/ppermute | solution.py:372
  278.5 22.9 %collective-permute-start.3 = (bf16[752,256]{1,0:T(8,128)(2,1)S(1)}, bf16[752,256]{1,0:T(8,128)(2,1)S(1)}, u32[]{:S(2)}, u32[]{:S(2)}) collective-permute-start(bf16[752,256]{1,0:T(8,128)(2,1)S(1)} %constant_dynamic-slice_fusion.2), channel_id=1, source_target_pairs={{0,24},{8,0},{16,8},{24,16},{1,25},{9,1},{17,9},{25,17},{2,26},{10... | collective-permute-start | bytes 1155080 | tf_op jit(solution)/shard_map/while/body/eval_jaxpr/ppermute | solution.py:372
  320.6 38.7 %all-to-all-start = ((bf16[32,64,128]{2,1,0:T(8,128)(2,1)}), bf16[32,64,128]{2,1,0:T(8,128)(2,1)S(1)}, u32[]{:S(2)}, u32[]{:S(2)}) async-start(bf16[32,64,128]{2,1,0:T(8,128)(2,1)} %get-tuple-element.935), calls=%async_computation | async-start | bytes 1048576 | tf_op jit(solution)/shard_map/while/body/eval_jaxpr/all_to_all | solution.py:293
  328.7 15.7 %collective-permute-start.1 = (bf16[752,256]{1,0:T(8,128)(2,1)S(1)}, bf16[752,256]{1,0:T(8,128)(2,1)S(1)}, u32[]{:S(2)}, u32[]{:S(2)}) collective-permute-start(bf16[752,256]{1,0:T(8,128)(2,1)S(1)} %constant_dynamic-slice_fusion.2), channel_id=1, source_target_pairs={{0,8},{8,16},{16,24},{24,0},{1,9},{9,17},{17,25},{25,1},{2,10},{10... | collective-permute-start | bytes 1155080 | tf_op jit(solution)/shard_map/while/body/eval_jaxpr/ppermute | solution.py:372
  330.0 23.8 %collective-permute-start.2 = (bf16[752,256]{1,0:T(8,128)(2,1)S(1)}, bf16[752,256]{1,0:T(8,128)(2,1)S(1)}, u32[]{:S(2)}, u32[]{:S(2)}) collective-permute-start(bf16[752,256]{1,0:T(8,128)(2,1)S(1)} %constant_dynamic-slice_fusion.2), channel_id=1, source_target_pairs={{0,16},{8,24},{16,0},{24,8},{1,17},{9,25},{17,1},{25,9},{2,18},{10... | collective-permute-start | bytes 1155080 | tf_op jit(solution)/shard_map/while/body/eval_jaxpr/ppermute | solution.py:372
  332.4 24.1 %collective-permute-start.3 = (bf16[752,256]{1,0:T(8,128)(2,1)S(1)}, bf16[752,256]{1,0:T(8,128)(2,1)S(1)}, u32[]{:S(2)}, u32[]{:S(2)}) collective-permute-start(bf16[752,256]{1,0:T(8,128)(2,1)S(1)} %constant_dynamic-slice_fusion.2), channel_id=1, source_target_pairs={{0,24},{8,0},{16,8},{24,16},{1,25},{9,1},{17,9},{25,17},{2,26},{10... | collective-permute-start | bytes 1155080 | tf_op jit(solution)/shard_map/while/body/eval_jaxpr/ppermute | solution.py:372
  373.2 37.7 %all-to-all-start = ((bf16[32,64,128]{2,1,0:T(8,128)(2,1)}), bf16[32,64,128]{2,1,0:T(8,128)(2,1)S(1)}, u32[]{:S(2)}, u32[]{:S(2)}) async-start(bf16[32,64,128]{2,1,0:T(8,128)(2,1)} %get-tuple-element.935), calls=%async_computation | async-start | bytes 1048576 | tf_op jit(solution)/shard_map/while/body/eval_jaxpr/all_to_all | solution.py:293
  381.4 14.4 %collective-permute-start.1 = (bf16[752,256]{1,0:T(8,128)(2,1)S(1)}, bf16[752,256]{1,0:T(8,128)(2,1)S(1)}, u32[]{:S(2)}, u32[]{:S(2)}) collective-permute-start(bf16[752,256]{1,0:T(8,128)(2,1)S(1)} %constant_dynamic-slice_fusion.2), channel_id=1, source_target_pairs={{0,8},{8,16},{16,24},{24,0},{1,9},{9,17},{17,25},{25,1},{2,10},{10... | collective-permute-start | bytes 1155080 | tf_op jit(solution)/shard_map/while/body/eval_jaxpr/ppermute | solution.py:372
  382.7 22.6 %collective-permute-start.2 = (bf16[752,256]{1,0:T(8,128)(2,1)S(1)}, bf16[752,256]{1,0:T(8,128)(2,1)S(1)}, u32[]{:S(2)}, u32[]{:S(2)}) collective-permute-start(bf16[752,256]{1,0:T(8,128)(2,1)S(1)} %constant_dynamic-slice_fusion.2), channel_id=1, source_target_pairs={{0,16},{8,24},{16,0},{24,8},{1,17},{9,25},{17,1},{25,9},{2,18},{10... | collective-permute-start | bytes 1155080 | tf_op jit(solution)/shard_map/while/body/eval_jaxpr/ppermute | solution.py:372
  385.1 23.0 %collective-permute-start.3 = (bf16[752,256]{1,0:T(8,128)(2,1)S(1)}, bf16[752,256]{1,0:T(8,128)(2,1)S(1)}, u32[]{:S(2)}, u32[]{:S(2)}) collective-permute-start(bf16[752,256]{1,0:T(8,128)(2,1)S(1)} %constant_dynamic-slice_fusion.2), channel_id=1, source_target_pairs={{0,24},{8,0},{16,8},{24,16},{1,25},{9,1},{17,9},{25,17},{2,26},{10... | collective-permute-start | bytes 1155080 | tf_op jit(solution)/shard_map/while/body/eval_jaxpr/ppermute | solution.py:372
  428.8 39.8 %all-to-all-start = ((bf16[32,64,128]{2,1,0:T(8,128)(2,1)}), bf16[32,64,128]{2,1,0:T(8,128)(2,1)S(1)}, u32[]{:S(2)}, u32[]{:S(2)}) async-start(bf16[32,64,128]{2,1,0:T(8,128)(2,1)} %get-tuple-element.935), calls=%async_computation | async-start | bytes 1048576 | tf_op jit(solution)/shard_map/while/body/eval_jaxpr/all_to_all | solution.py:293
  438.9 16.3 %collective-permute-start.1 = (bf16[752,256]{1,0:T(8,128)(2,1)S(1)}, bf16[752,256]{1,0:T(8,128)(2,1)S(1)}, u32[]{:S(2)}, u32[]{:S(2)}) collective-permute-start(bf16[752,256]{1,0:T(8,128)(2,1)S(1)} %constant_dynamic-slice_fusion.2), channel_id=1, source_target_pairs={{0,8},{8,16},{16,24},{24,0},{1,9},{9,17},{17,25},{25,1},{2,10},{10... | collective-permute-start | bytes 1155080 | tf_op jit(solution)/shard_map/while/body/eval_jaxpr/ppermute | solution.py:372
  440.2 22.9 %collective-permute-start.2 = (bf16[752,256]{1,0:T(8,128)(2,1)S(1)}, bf16[752,256]{1,0:T(8,128)(2,1)S(1)}, u32[]{:S(2)}, u32[]{:S(2)}) collective-permute-start(bf16[752,256]{1,0:T(8,128)(2,1)S(1)} %constant_dynamic-slice_fusion.2), channel_id=1, source_target_pairs={{0,16},{8,24},{16,0},{24,8},{1,17},{9,25},{17,1},{25,9},{2,18},{10... | collective-permute-start | bytes 1155080 | tf_op jit(solution)/shard_map/while/body/eval_jaxpr/ppermute | solution.py:372
  442.7 23.2 %collective-permute-start.3 = (bf16[752,256]{1,0:T(8,128)(2,1)S(1)}, bf16[752,256]{1,0:T(8,128)(2,1)S(1)}, u32[]{:S(2)}, u32[]{:S(2)}) collective-permute-start(bf16[752,256]{1,0:T(8,128)(2,1)S(1)} %constant_dynamic-slice_fusion.2), channel_id=1, source_target_pairs={{0,24},{8,0},{16,8},{24,16},{1,25},{9,1},{17,9},{25,17},{2,26},{10... | collective-permute-start | bytes 1155080 | tf_op jit(solution)/shard_map/while/body/eval_jaxpr/ppermute | solution.py:372
  482.9 39.4 %all-to-all-start = ((bf16[32,64,128]{2,1,0:T(8,128)(2,1)}), bf16[32,64,128]{2,1,0:T(8,128)(2,1)S(1)}, u32[]{:S(2)}, u32[]{:S(2)}) async-start(bf16[32,64,128]{2,1,0:T(8,128)(2,1)} %get-tuple-element.935), calls=%async_computation | async-start | bytes 1048576 | tf_op jit(solution)/shard_map/while/body/eval_jaxpr/all_to_all | solution.py:293
  491.1 16.2 %collective-permute-start.1 = (bf16[752,256]{1,0:T(8,128)(2,1)S(1)}, bf16[752,256]{1,0:T(8,128)(2,1)S(1)}, u32[]{:S(2)}, u32[]{:S(2)}) collective-permute-start(bf16[752,256]{1,0:T(8,128)(2,1)S(1)} %constant_dynamic-slice_fusion.2), channel_id=1, source_target_pairs={{0,8},{8,16},{16,24},{24,0},{1,9},{9,17},{17,25},{25,1},{2,10},{10... | collective-permute-start | bytes 1155080 | tf_op jit(solution)/shard_map/while/body/eval_jaxpr/ppermute | solution.py:372
  492.4 24.3 %collective-permute-start.2 = (bf16[752,256]{1,0:T(8,128)(2,1)S(1)}, bf16[752,256]{1,0:T(8,128)(2,1)S(1)}, u32[]{:S(2)}, u32[]{:S(2)}) collective-permute-start(bf16[752,256]{1,0:T(8,128)(2,1)S(1)} %constant_dynamic-slice_fusion.2), channel_id=1, source_target_pairs={{0,16},{8,24},{16,0},{24,8},{1,17},{9,25},{17,1},{25,9},{2,18},{10... | collective-permute-start | bytes 1155080 | tf_op jit(solution)/shard_map/while/body/eval_jaxpr/ppermute | solution.py:372
  494.9 24.7 %collective-permute-start.3 = (bf16[752,256]{1,0:T(8,128)(2,1)S(1)}, bf16[752,256]{1,0:T(8,128)(2,1)S(1)}, u32[]{:S(2)}, u32[]{:S(2)}) collective-permute-start(bf16[752,256]{1,0:T(8,128)(2,1)S(1)} %constant_dynamic-slice_fusion.2), channel_id=1, source_target_pairs={{0,24},{8,0},{16,8},{24,16},{1,25},{9,1},{17,9},{25,17},{2,26},{10... | collective-permute-start | bytes 1155080 | tf_op jit(solution)/shard_map/while/body/eval_jaxpr/ppermute | solution.py:372
  534.6 37.4 %all-to-all-start = ((bf16[32,64,128]{2,1,0:T(8,128)(2,1)}), bf16[32,64,128]{2,1,0:T(8,128)(2,1)S(1)}, u32[]{:S(2)}, u32[]{:S(2)}) async-start(bf16[32,64,128]{2,1,0:T(8,128)(2,1)} %get-tuple-element.935), calls=%async_computation | async-start | bytes 1048576 | tf_op jit(solution)/shard_map/while/body/eval_jaxpr/all_to_all | solution.py:293
  544.2 22.3 %collective-permute-start.2 = (bf16[752,256]{1,0:T(8,128)(2,1)S(1)}, bf16[752,256]{1,0:T(8,128)(2,1)S(1)}, u32[]{:S(2)}, u32[]{:S(2)}) collective-permute-start(bf16[752,256]{1,0:T(8,128)(2,1)S(1)} %constant_dynamic-slice_fusion.2), channel_id=1, source_target_pairs={{0,16},{8,24},{16,0},{24,8},{1,17},{9,25},{17,1},{25,9},{2,18},{10... | collective-permute-start | bytes 1155080 | tf_op jit(solution)/shard_map/while/body/eval_jaxpr/ppermute | solution.py:372
  546.6 22.6 %collective-permute-start.3 = (bf16[752,256]{1,0:T(8,128)(2,1)S(1)}, bf16[752,256]{1,0:T(8,128)(2,1)S(1)}, u32[]{:S(2)}, u32[]{:S(2)}) collective-permute-start(bf16[752,256]{1,0:T(8,128)(2,1)S(1)} %constant_dynamic-slice_fusion.2), channel_id=1, source_target_pairs={{0,24},{8,0},{16,8},{24,16},{1,25},{9,1},{17,9},{25,17},{2,26},{10... | collective-permute-start | bytes 1155080 | tf_op jit(solution)/shard_map/while/body/eval_jaxpr/ppermute | solution.py:372
  587.7 37.7 %all-to-all-start = ((bf16[32,64,128]{2,1,0:T(8,128)(2,1)}), bf16[32,64,128]{2,1,0:T(8,128)(2,1)S(1)}, u32[]{:S(2)}, u32[]{:S(2)}) async-start(bf16[32,64,128]{2,1,0:T(8,128)(2,1)} %get-tuple-element.935), calls=%async_computation | async-start | bytes 1048576 | tf_op jit(solution)/shard_map/while/body/eval_jaxpr/all_to_all | solution.py:293
  596.0 14.4 %collective-permute-start.1 = (bf16[752,256]{1,0:T(8,128)(2,1)S(1)}, bf16[752,256]{1,0:T(8,128)(2,1)S(1)}, u32[]{:S(2)}, u32[]{:S(2)}) collective-permute-start(bf16[752,256]{1,0:T(8,128)(2,1)S(1)} %constant_dynamic-slice_fusion.2), channel_id=1, source_target_pairs={{0,8},{8,16},{16,24},{24,0},{1,9},{9,17},{17,25},{25,1},{2,10},{10... | collective-permute-start | bytes 1155080 | tf_op jit(solution)/shard_map/while/body/eval_jaxpr/ppermute | solution.py:372
  597.2 22.6 %collective-permute-start.2 = (bf16[752,256]{1,0:T(8,128)(2,1)S(1)}, bf16[752,256]{1,0:T(8,128)(2,1)S(1)}, u32[]{:S(2)}, u32[]{:S(2)}) collective-permute-start(bf16[752,256]{1,0:T(8,128)(2,1)S(1)} %constant_dynamic-slice_fusion.2), channel_id=1, source_target_pairs={{0,16},{8,24},{16,0},{24,8},{1,17},{9,25},{17,1},{25,9},{2,18},{10... | collective-permute-start | bytes 1155080 | tf_op jit(solution)/shard_map/while/body/eval_jaxpr/ppermute | solution.py:372
  599.7 22.9 %collective-permute-start.3 = (bf16[752,256]{1,0:T(8,128)(2,1)S(1)}, bf16[752,256]{1,0:T(8,128)(2,1)S(1)}, u32[]{:S(2)}, u32[]{:S(2)}) collective-permute-start(bf16[752,256]{1,0:T(8,128)(2,1)S(1)} %constant_dynamic-slice_fusion.2), channel_id=1, source_target_pairs={{0,24},{8,0},{16,8},{24,16},{1,25},{9,1},{17,9},{25,17},{2,26},{10... | collective-permute-start | bytes 1155080 | tf_op jit(solution)/shard_map/while/body/eval_jaxpr/ppermute | solution.py:372
  650.0 16.8 %all-to-all-start.1 = ((bf16[8,2,64,128]{3,2,1,0:T(8,128)(2,1)}), bf16[8,2,64,128]{3,2,1,0:T(8,128)(2,1)S(1)}, u32[]{:S(2)}, u32[]{:S(2)}) async-start(bf16[8,2,64,128]{3,2,1,0:T(8,128)(2,1)} %get-tuple-element.954), calls=%async_computation.1 | async-start | bytes 524288 | tf_op jit(solution)/shard_map/while/body/eval_jaxpr/all_to_all | solution.py:407
  718.1 15.6 %all-to-all-start.1 = ((bf16[8,2,64,128]{3,2,1,0:T(8,128)(2,1)}), bf16[8,2,64,128]{3,2,1,0:T(8,128)(2,1)S(1)}, u32[]{:S(2)}, u32[]{:S(2)}) async-start(bf16[8,2,64,128]{3,2,1,0:T(8,128)(2,1)} %get-tuple-element.954), calls=%async_computation.1 | async-start | bytes 524288 | tf_op jit(solution)/shard_map/while/body/eval_jaxpr/all_to_all | solution.py:407
  750.3 14.8 %all-to-all-start.1 = ((bf16[8,2,64,128]{3,2,1,0:T(8,128)(2,1)}), bf16[8,2,64,128]{3,2,1,0:T(8,128)(2,1)S(1)}, u32[]{:S(2)}, u32[]{:S(2)}) async-start(bf16[8,2,64,128]{3,2,1,0:T(8,128)(2,1)} %get-tuple-element.954), calls=%async_computation.1 | async-start | bytes 524288 | tf_op jit(solution)/shard_map/while/body/eval_jaxpr/all_to_all | solution.py:407
  812.4 14.0 %all-to-all-start.1 = ((bf16[8,2,64,128]{3,2,1,0:T(8,128)(2,1)}), bf16[8,2,64,128]{3,2,1,0:T(8,128)(2,1)S(1)}, u32[]{:S(2)}, u32[]{:S(2)}) async-start(bf16[8,2,64,128]{3,2,1,0:T(8,128)(2,1)} %get-tuple-element.954), calls=%async_computation.1 | async-start | bytes 524288 | tf_op jit(solution)/shard_map/while/body/eval_jaxpr/all_to_all | solution.py:407
  843.0 14.0 %all-to-all-start.1 = ((bf16[8,2,64,128]{3,2,1,0:T(8,128)(2,1)}), bf16[8,2,64,128]{3,2,1,0:T(8,128)(2,1)S(1)}, u32[]{:S(2)}, u32[]{:S(2)}) async-start(bf16[8,2,64,128]{3,2,1,0:T(8,128)(2,1)} %get-tuple-element.954), calls=%async_computation.1 | async-start | bytes 524288 | tf_op jit(solution)/shard_map/while/body/eval_jaxpr/all_to_all | solution.py:407
  (38 other events, 323.9 us)
